TPU v7x, 32 devices: a whole 2x2x4 slice. The times are simulated.
32 devices in a mesh: batch: 8 (over z, x), mlp: 4 (over y, core).
Axes of the slice: x: 2, y: 2, z: 4, core: 2. Of those that a mesh axis runs over, the one named last changes fastest.
Arguments:
- patches: bfloat16 [128, 196, 768], P(('batch', 'mlp')), may hold values from -6 to 6
- mask: int32 [128, 196], P(('batch', 'mlp')), may hold values from 0 to 1, as said below
- student_square: float32 [3, 768, 768], P(None, 'batch')
- student_qkv: float32 [768, 2304], P('batch'), may hold values from -0.21875 to 0.21875
- student_expand: float32 [768, 3072], P('batch'), may hold values from -0.21875 to 0.21875
- student_contract: float32 [3072, 768], P('batch'), may hold values from -0.109375 to 0.109375
- student_vectors: float32 [17, 768], P(None, 'batch')
- first_square: float32 [3, 768, 768], P(None, 'batch')
- first_qkv: float32 [768, 2304], P('batch')
- first_expand: float32 [768, 3072], P('batch')
- first_contract: float32 [3072, 768], P('batch')
- first_vectors: float32 [17, 768], P(None, 'batch')
- second_square: float32 [3, 768, 768], P(None, 'batch'), as said below
- second_qkv: float32 [768, 2304], P('batch'), as said below
- second_expand: float32 [768, 3072], P('batch'), as said below
- second_contract: float32 [3072, 768], P('batch'), as said below
- second_vectors: float32 [17, 768], P(None, 'batch'), as said below
- teacher_square: bfloat16 [2, 768, 768], replicated
- teacher_qkv: bfloat16 [768, 2304], replicated, may hold values from -0.21875 to 0.21875
- teacher_expand: bfloat16 [768, 3072], P(None, 'mlp'), may hold values from -0.21875 to 0.21875
- teacher_contract: bfloat16 [3072, 768], P('mlp'), may hold values from -0.109375 to 0.109375
- teacher_vectors: float32 [13, 768], replicated
Outputs:
- loss_sum: float32 [], replicated
- masked_count: float32 [], replicated
- grad_norm: float32 [], replicated
- moment_square: float32 [3, 768, 768], P(None, 'batch')
- variance_square: float32 [3, 768, 768], P(None, 'batch')
- updated_square: float32 [3, 768, 768], P(None, 'batch')
- moment_qkv: float32 [768, 2304], P('batch')
- variance_qkv: float32 [768, 2304], P('batch')
- updated_qkv: float32 [768, 2304], P('batch')
- moment_expand: float32 [768, 3072], P('batch')
- variance_expand: float32 [768, 3072], P('batch')
- updated_expand: float32 [768, 3072], P('batch')
- moment_contract: float32 [3072, 768], P('batch')
- variance_contract: float32 [3072, 768], P('batch')
- updated_contract: float32 [3072, 768], P('batch')
- moment_vectors: float32 [17, 768], P(None, 'batch')
- variance_vectors: float32 [17, 768], P(None, 'batch')
- updated_vectors: float32 [17, 768], P(None, 'batch')
Inputs may be any that keep to these rules, and one draw needn't show every extreme that they name: `mask`: each image has between 40 and 80 percent of its 196 patches masked. `second_square`: positive. `second_qkv`: positive. `second_expand`: positive. `second_contract`: positive. `second_vectors`: positive.
All inputs are finite; a program needn't handle non-finite values.
Results may differ from a plain program's by a relative error of at most 0.0019.
The roundings to bfloat16 on the way count: a program that leaves them out, or rounds other values in their place, can miss the bound.
Values may be sent and summed in bfloat16 or wider, within the bound.
No kernel may reach another device: no remote copies, remote signals or barrier semaphores. Data moves between devices by JAX's collectives and lax.ppermute only.
A program may use at most 192 MiB of HBM per device.

v0:
```python
import jax
import jax.numpy as jnp
from jax import lax
from jax.sharding import PartitionSpec as P

D = 768
HEAD_DIM = 64
STEP = 10


norm_eps = 1e-06
inst_eps = 1e-05
clip_bound = 0.001
rate_matrix = 0.05
rate_vector = 0.5
decay_matrix = 0.05
beta_first = 0.9
beta_second = 0.999
adam_eps = 1e-08


def product(left, right):
    return jnp.dot(left, right, preferred_element_type=jnp.float32)


def weight_grad(inputs, grads_low):
    return jnp.einsum("gri,grj->ij", inputs, grads_low, preferred_element_type=jnp.float32)


def back_product(grads_low, matrix):
    return jnp.einsum("grj,ij->gri", grads_low, matrix, preferred_element_type=jnp.float32)


def column_sum(grads_low):
    return jnp.sum(grads_low.astype(jnp.float32), axis=(0, 1))


def norm_rows(values, gain, shift):
    centred = values - jnp.mean(values, axis=-1, keepdims=True)
    variance = jnp.mean(centred * centred, axis=-1, keepdims=True)
    return centred * lax.rsqrt(variance + norm_eps) * gain + shift


def inst_norm(values):
    centred = values - jnp.mean(values, axis=1, keepdims=True)
    variance = jnp.mean(centred * centred, axis=1, keepdims=True)
    return centred * lax.rsqrt(variance + inst_eps)


def gelu_exact(values):
    return jax.nn.gelu(values, approximate=False)


def split_heads(values):
    return values.reshape(values.shape[0], values.shape[1], -1, HEAD_DIM)


def joint_bias(query_bias, value_bias):
    return jnp.concatenate([query_bias, jnp.zeros_like(query_bias), value_bias])


def split_joint(mixed):
    width = mixed.shape[-1] // 3
    low_mixed = mixed.astype(jnp.bfloat16)
    return (low_mixed[..., :width], low_mixed[..., width : 2 * width], low_mixed[..., 2 * width :])


def score_block(queries, key_rows):
    return jnp.einsum(
        "gqhd,gkhd->ghqk",
        split_heads(queries),
        split_heads(key_rows),
        preferred_element_type=jnp.float32,
    ) * HEAD_DIM ** (-0.5)


def attention_forward(queries, key_rows, value_rows):
    scores = score_block(queries, key_rows)
    row_max = jnp.max(scores, axis=-1, keepdims=True)
    shifted = jnp.exp(scores - row_max)
    row_total = jnp.sum(shifted, axis=-1, keepdims=True)
    probs = (shifted / row_total).astype(jnp.bfloat16)
    log_total = row_max + jnp.log(row_total)
    mixed = jnp.einsum(
        "ghqk,gkhd->gqhd", probs, split_heads(value_rows), preferred_element_type=jnp.float32
    )
    return (mixed.reshape(queries.shape), log_total)


def attention_backward(queries, key_rows, value_rows, log_total, d_attended):
    probs = jnp.exp(score_block(queries, key_rows) - log_total)
    grad_heads = split_heads(d_attended)
    d_values = jnp.einsum(
        "ghqk,gqhd->gkhd",
        probs.astype(jnp.bfloat16),
        grad_heads,
        preferred_element_type=jnp.float32,
    )
    d_probs = jnp.einsum(
        "gqhd,gkhd->ghqk", grad_heads, split_heads(value_rows), preferred_element_type=jnp.float32
    )
    d_scores = (probs * (d_probs - jnp.sum(probs * d_probs, axis=-1, keepdims=True))).astype(
        jnp.bfloat16
    )
    d_queries = jnp.einsum(
        "ghqk,gkhd->gqhd", d_scores, split_heads(key_rows), preferred_element_type=jnp.float32
    ) * HEAD_DIM ** (-0.5)
    d_keys = jnp.einsum(
        "ghqk,gqhd->gkhd", d_scores, split_heads(queries), preferred_element_type=jnp.float32
    ) * HEAD_DIM ** (-0.5)
    full_shape = queries.shape
    return jnp.concatenate(
        [d_queries.reshape(full_shape), d_keys.reshape(full_shape), d_values.reshape(full_shape)],
        axis=-1,
    )


def teacher_targets(pixels, teacher_square, teacher_qkv, teacher_expand, teacher_contract, vectors):
    embed = product(pixels, teacher_square[0]) + vectors[0]
    normed = norm_rows(embed, vectors[1], vectors[2]).astype(jnp.bfloat16)
    queries, key_rows, value_rows = split_joint(
        product(normed, teacher_qkv) + joint_bias(vectors[3], vectors[4])
    )
    attended, _ = attention_forward(queries, key_rows, value_rows)
    middle = embed + product(attended.astype(jnp.bfloat16), teacher_square[1]) + vectors[5]
    normed_two = norm_rows(middle, vectors[6], vectors[7]).astype(jnp.bfloat16)
    flat_rows = normed_two.reshape(-1, normed_two.shape[-1])
    bias_all = vectors[8:12].reshape(-1)
    width = teacher_expand.shape[1]
    bias_part = lax.dynamic_slice_in_dim(bias_all, lax.axis_index("mlp") * width, width)
    hidden = gelu_exact(
        product(lax.all_gather(flat_rows, "mlp", axis=0, tiled=True), teacher_expand) + bias_part
    ).astype(jnp.bfloat16)
    output = lax.psum_scatter(
        product(hidden, teacher_contract), "mlp", scatter_dimension=0, tiled=True
    )
    output = output.reshape(middle.shape) + vectors[12]
    return 0.5 * (inst_norm(middle) + inst_norm(output))


def student_forward(weights, pixels, marks, targets):
    square, joint, expand, contract, vectors_low = weights
    vectors = vectors_low.astype(jnp.float32)
    embed = product(pixels, square[0]) + vectors[0]
    start = jnp.where(marks[..., None] > 0, vectors[1], embed)
    normed = norm_rows(start, vectors[2], vectors[3]).astype(jnp.bfloat16)
    queries, key_rows, value_rows = split_joint(
        product(normed, joint) + joint_bias(vectors[4], vectors[5])
    )
    attended, log_total = attention_forward(queries, key_rows, value_rows)
    attended = attended.astype(jnp.bfloat16)
    middle = start + product(attended, square[1]) + vectors[6]
    normed_two = norm_rows(middle, vectors[7], vectors[8]).astype(jnp.bfloat16)
    pre_act = product(normed_two, expand) + vectors[9:13].reshape(-1)
    hidden = gelu_exact(pre_act).astype(jnp.bfloat16)
    final = middle + product(hidden, contract) + vectors[13]
    normed_three = norm_rows(final, vectors[14], vectors[15]).astype(jnp.bfloat16)
    error = product(normed_three, square[2]) + vectors[16] - targets
    loss_part = jnp.sum(marks[..., None] * error * error)
    stored = (
        start,
        normed,
        queries,
        key_rows,
        value_rows,
        log_total,
        attended,
        middle,
        normed_two,
        pre_act,
        hidden,
        final,
        normed_three,
        error,
    )
    return (loss_part, stored)


def student_backward(weights, pixels, marks, stored, loss_scale):
    square, joint, expand, contract, vectors_low = weights
    vectors = vectors_low.astype(jnp.float32)
    (
        start,
        normed,
        queries,
        key_rows,
        value_rows,
        log_total,
        attended,
        middle,
        normed_two,
        pre_act,
        hidden,
        final,
        normed_three,
        error,
    ) = stored
    d_pred = (marks[..., None] * error * loss_scale).astype(jnp.bfloat16)
    grad_head = weight_grad(normed_three, d_pred)
    bias_head = column_sum(d_pred)
    _, final_back = jax.vjp(norm_rows, final, vectors[14], vectors[15])
    d_final, gain_final, shift_final = final_back(back_product(d_pred, square[2]))
    d_branch = d_final.astype(jnp.bfloat16)
    grad_contract = weight_grad(hidden, d_branch)
    bias_contract = column_sum(d_branch)
    _, act_back = jax.vjp(gelu_exact, pre_act)
    d_pre = act_back(back_product(d_branch, contract))[0].astype(jnp.bfloat16)
    grad_expand = weight_grad(normed_two, d_pre)
    bias_expand = column_sum(d_pre)
    _, middle_back = jax.vjp(norm_rows, middle, vectors[7], vectors[8])
    d_middle_part, gain_two, shift_two = middle_back(back_product(d_pre, expand))
    d_middle = d_final + d_middle_part
    d_attn = d_middle.astype(jnp.bfloat16)
    grad_out = weight_grad(attended, d_attn)
    bias_out = column_sum(d_attn)
    d_attended = back_product(d_attn, square[1]).astype(jnp.bfloat16)
    d_joint = attention_backward(queries, key_rows, value_rows, log_total, d_attended).astype(
        jnp.bfloat16
    )
    grad_joint = weight_grad(normed, d_joint)
    bias_joint = column_sum(d_joint)
    width = bias_joint.shape[0] // 3
    _, start_back = jax.vjp(norm_rows, start, vectors[2], vectors[3])
    d_start_part, gain_one, shift_one = start_back(back_product(d_joint, joint))
    d_start = d_middle + d_start_part
    is_masked = marks[..., None] > 0
    mask_grad = jnp.sum(jnp.where(is_masked, d_start, 0.0), axis=(0, 1))
    d_embed = jnp.where(is_masked, 0.0, d_start).astype(jnp.bfloat16)
    grad_embed = weight_grad(pixels, d_embed)
    bias_embed = column_sum(d_embed)
    head_rows = jnp.stack(
        [
            bias_embed,
            mask_grad,
            gain_one,
            shift_one,
            bias_joint[:width],
            bias_joint[2 * width :],
            bias_out,
            gain_two,
            shift_two,
        ]
    )
    tail_rows = jnp.stack([bias_contract, gain_final, shift_final, bias_head])
    vector_grad = jnp.concatenate([head_rows, bias_expand.reshape(4, -1), tail_rows], axis=0)
    return (
        jnp.stack([grad_embed, grad_out, grad_head]),
        grad_joint,
        grad_expand,
        grad_contract,
        vector_grad,
    )


def square_total(grads):
    total = jnp.zeros((), jnp.float32)
    for member in grads:
        total = total + jnp.sum(member * member)
    return total


def adam_update(master, first, second, gradient, step_rate, weight_decay):
    moment = beta_first * first + (1.0 - beta_first) * gradient
    variance = beta_second * second + (1.0 - beta_second) * gradient * gradient
    corrected = moment / (1.0 - beta_first**STEP)
    scaled = variance / (1.0 - beta_second**STEP)
    updated = master - step_rate * (
        corrected / (jnp.sqrt(scaled) + adam_eps) + weight_decay * master
    )
    return (moment, variance, updated)


def on_device(
    patches,
    mask,
    student_square,
    student_qkv,
    student_expand,
    student_contract,
    student_vectors,
    first_square,
    first_qkv,
    first_expand,
    first_contract,
    first_vectors,
    second_square,
    second_qkv,
    second_expand,
    second_contract,
    second_vectors,
    teacher_square,
    teacher_qkv,
    teacher_expand,
    teacher_contract,
    teacher_vectors,
):
    weights = (
        lax.all_gather(student_square.astype(jnp.bfloat16), "batch", axis=1, tiled=True),
        lax.all_gather(student_qkv.astype(jnp.bfloat16), "batch", axis=0, tiled=True),
        lax.all_gather(student_expand.astype(jnp.bfloat16), "batch", axis=0, tiled=True),
        lax.all_gather(student_contract.astype(jnp.bfloat16), "batch", axis=0, tiled=True),
        lax.all_gather(student_vectors.astype(jnp.bfloat16), "batch", axis=1, tiled=True),
    )
    marks = mask.astype(jnp.float32)
    masked_count = lax.psum(jnp.sum(marks), ("batch", "mlp"))
    targets = teacher_targets(
        patches, teacher_square, teacher_qkv, teacher_expand, teacher_contract, teacher_vectors
    )
    loss_part, stored = student_forward(weights, patches, marks, targets)
    loss_sum = lax.psum(loss_part, ("batch", "mlp"))
    local = student_backward(weights, patches, marks, stored, 2.0 / (masked_count * D))
    shared = (
        lax.psum_scatter(local[0], "batch", scatter_dimension=1, tiled=True),
        lax.psum_scatter(local[1], "batch", scatter_dimension=0, tiled=True),
        lax.psum_scatter(local[2], "batch", scatter_dimension=0, tiled=True),
        lax.psum_scatter(local[3], "batch", scatter_dimension=0, tiled=True),
        lax.psum_scatter(local[4], "batch", scatter_dimension=1, tiled=True),
    )
    grads = lax.psum((shared[0], shared[1], shared[2], shared[3], shared[4]), "mlp")
    grad_squares = lax.psum(square_total(grads), "batch")
    grad_norm = jnp.sqrt(grad_squares)
    factor = clip_bound / jnp.maximum(grad_norm, clip_bound)
    moment_square, variance_square, updated_square = adam_update(
        student_square, first_square, second_square, grads[0] * factor, rate_matrix, decay_matrix
    )
    moment_qkv, variance_qkv, updated_qkv = adam_update(
        student_qkv, first_qkv, second_qkv, grads[1] * factor, rate_matrix, decay_matrix
    )
    moment_expand, variance_expand, updated_expand = adam_update(
        student_expand, first_expand, second_expand, grads[2] * factor, rate_matrix, decay_matrix
    )
    moment_contract, variance_contract, updated_contract = adam_update(
        student_contract,
        first_contract,
        second_contract,
        grads[3] * factor,
        rate_matrix,
        decay_matrix,
    )
    moment_vectors, variance_vectors, updated_vectors = adam_update(
        student_vectors, first_vectors, second_vectors, grads[4] * factor, rate_vector, 0.0
    )
    return (
        loss_sum,
        masked_count,
        grad_norm,
        moment_square,
        variance_square,
        updated_square,
        moment_qkv,
        variance_qkv,
        updated_qkv,
        moment_expand,
        variance_expand,
        updated_expand,
        moment_contract,
        variance_contract,
        updated_contract,
        moment_vectors,
        variance_vectors,
        updated_vectors,
    )


def solution(mesh):
    return jax.shard_map(
        on_device,
        mesh=mesh,
        in_specs=(
            P(("batch", "mlp"), None, None),
            P(("batch", "mlp"), None),
            P(None, "batch", None),
            P("batch", None),
            P("batch", None),
            P("batch", None),
            P(None, "batch"),
            P(None, "batch", None),
            P("batch", None),
            P("batch", None),
            P("batch", None),
            P(None, "batch"),
            P(None, "batch", None),
            P("batch", None),
            P("batch", None),
            P("batch", None),
            P(None, "batch"),
            P(),
            P(),
            P(None, "mlp"),
            P("mlp", None),
            P(),
        ),
        out_specs=(
            P(),
            P(),
            P(),
            P(None, "batch", None),
            P(None, "batch", None),
            P(None, "batch", None),
            P("batch", None),
            P("batch", None),
            P("batch", None),
            P("batch", None),
            P("batch", None),
            P("batch", None),
            P("batch", None),
            P("batch", None),
            P("batch", None),
            P(None, "batch"),
            P(None, "batch"),
            P(None, "batch"),
        ),
        check_vma=False,
    )
```

profile of v0, /device:TPU:0, one launch (start us, length us, event | category | flops | bytes accessed | tf_op | source)
XLA Modules:
  0.0 1468.8 jit_solution(5068930527564302015)
XLA Ops:
  9.8 32.4 %all-gather = bf16[8,96,17]{1,2,0:T(8,128)(2,1)S(1)} all-gather(bf16[1,96,17]{1,2,0:T(8,128)(2,1)S(1)} %convert_bitcast_fusion), channel_id=1, replica_groups=mesh['batch'=8,'mlp'=4] {'batch'}, dimensions={0}, use_global_device_ids=true | all-gather | bytes 29376 | tf_op jit(solution)/shard_map/all_gather | solution.py:302
  61.2 8.8 fusion.131
  87.0 33.9 %all-gather.15.cloned.1.call-done = bf16[3136,768]{1,0:T(8,128)(2,1)} async-done(((bf16[784,768]{1,0:T(8,128)(2,1)}), bf16[3136,768]{1,0:T(8,128)(2,1)}) %all-gather.15.cloned.1.call-update) | async-done | bytes 4816912 | tf_op jit(solution)/shard_map/all_gather | solution.py:132
  120.9 31.8 %fusion.40 = f32[3136,768]{1,0:T(8,128)} fusion(bf16[768,768]{1,0:T(8,128)(2,1)S(1)} %copy-done.71, bf16[3136,768]{1,0:T(8,128)(2,1)} %all-gather.15.cloned.1.call-done, bf16[768,768]{1,0:T(8,128)(2,1)} %param.41, f32[768]{0:T(1024)S(1)} %dynamic_slice.3), kind=kOutput, calls=%fused_computation.86 | convolution fusion | flops 7557709824 | bytes 16813056 | tf_op jit(solution)/shard_map/dot_general | solution.py:23
  154.2 34.7 %all-gather.7.cloned.1.call-done = bf16[3,768,768]{2,1,0:T(8,128)(2,1)} async-done(((bf16[3,96,768]{2,1,0:T(8,128)(2,1)}), bf16[3,768,768]{2,1,0:T(8,128)(2,1)}) %all-gather.7.cloned.1.call-update) | async-done | bytes 3538960 | tf_op jit(solution)/shard_map/all_gather | solution.py:298
  192.5 62.8 %all-gather.9.cloned.1.call-done = bf16[768,2304]{1,0:T(8,128)(2,1)} async-done(((bf16[96,2304]{1,0:T(8,128)(2,1)}), bf16[768,2304]{1,0:T(8,128)(2,1)}) %all-gather.9.cloned.1.call-update) | async-done | bytes 3538960 | tf_op jit(solution)/shard_map/all_gather | solution.py:299
  281.6 54.7 %all-gather.11.cloned.1.call-done = bf16[768,3072]{1,0:T(8,128)(2,1)} async-done(((bf16[96,3072]{1,0:T(8,128)(2,1)}), bf16[768,3072]{1,0:T(8,128)(2,1)}) %all-gather.11.cloned.1.call-update) | async-done | bytes 4718608 | tf_op jit(solution)/shard_map/all_gather | solution.py:300
  336.4 9.1 fusion.44
  349.1 23.7 %multiply_convert_fusion.1 = (bf16[4,196,3072]{2,1,0:T(8,128)(2,1)}, f32[4,196,3072]{2,1,0:T(8,128)}) fusion(f32[4,196,3072]{2,1,0:T(8,128)S(1)} %get-tuple-element.168, f32[3072]{0:T(1024)S(1)} %add.380, u8[196,3072]{1,0:T(8,128)(4,1)S(1)} %get-tuple-element.73, u8[196,3072]{1,0:T(8,128)(4,1)S(1)} %get-tuple-element.72), kind=kLoop, calls=%fused_computation.16 | loop fusion | flops 170999808 | bytes 25300992 | tf_op jit(solution)/shard_map/convert_element_type | solution.py:155
  372.8 44.2 %all-gather.13.cloned.1.call-done = bf16[3072,768]{1,0:T(8,128)(2,1)} async-done(((bf16[384,768]{1,0:T(8,128)(2,1)}), bf16[3072,768]{1,0:T(8,128)(2,1)}) %all-gather.13.cloned.1.call-update) | async-done | bytes 4718608 | tf_op jit(solution)/shard_map/all_gather | solution.py:301
  417.0 7.5 fusion.133
  426.4 70.9 %reduce-scatter.11.cloned.1.call-done = f32[784,768]{1,0:T(8,128)} async-done(((f32[3136,768]{1,0:T(8,128)}), f32[784,768]{1,0:T(8,128)}) %reduce-scatter.11.cloned.1.call-update) | async-done | bytes 2408464 | tf_op jit(solution)/shard_map/reduce_scatter | solution.py:134
  509.6 39.6 %all-reduce = (f32[]{:T(128)}, f32[]{:T(128)}) all-reduce(f32[]{:T(128)} %get-tuple-element.171, f32[]{:T(128)} %convert_reduce_fusion.6), channel_id=1, replica_groups=mesh['batch'=8,'mlp'=4] {'batch','mlp'}, use_global_device_ids=true, to_apply=%region_20.21 | all-reduce | flops 2 | bytes 16 | tf_op jit(solution)/shard_map/psum | solution.py:310
  560.6 12.2 convert_reduce_fusion
  572.8 7.7 fusion.117
  592.1 7.4 fusion.49
  599.6 7.5 multiply_reduce_fusion
  607.0 11.5 multiply_convert_fusion
  634.0 7.1 multiply_reduce_fusion.5
  649.8 11.0 copy.173
  660.8 8.2 copy.178
  669.7 9.9 convolution_bitcast_fusion
  679.6 10.5 convolution_bitcast_fusion.2
  691.4 9.8 convolution_bitcast_fusion.1
  705.8 93.3 %reduce-scatter.19.cloned.1.call-done = f32[96,2304]{1,0:T(8,128)} async-done(((f32[768,2304]{1,0:T(8,128)}), f32[96,2304]{1,0:T(8,128)}) %reduce-scatter.19.cloned.1.call-update) | async-done | bytes 884752
  801.8 129.5 %reduce-scatter.13.cloned.1.call-done = f32[96,2304]{1,0:T(8,128)} async-done(((f32[768,2304]{1,0:T(8,128)}), f32[96,2304]{1,0:T(8,128)}) %reduce-scatter.13.cloned.1.call-update) | async-done | bytes 884752 | tf_op jit(solution)/shard_map/reduce_scatter | solution.py:314
  931.4 166.1 %reduce-scatter.15.cloned.1.call-done = f32[96,3072]{1,0:T(8,128)} async-done(((f32[768,3072]{1,0:T(8,128)}), f32[96,3072]{1,0:T(8,128)}) %reduce-scatter.15.cloned.1.call-update) | async-done | bytes 1179664 | tf_op jit(solution)/shard_map/reduce_scatter | solution.py:315
  1097.5 166.0 %reduce-scatter.17.cloned.1.call-done = f32[384,768]{1,0:T(8,128)} async-done(((f32[3072,768]{1,0:T(8,128)}), f32[384,768]{1,0:T(8,128)}) %reduce-scatter.17.cloned.1.call-update) | async-done | bytes 1179664 | tf_op jit(solution)/shard_map/reduce_scatter | solution.py:316
  1263.6 64.3 %reduce-scatter.21.cloned.1.call-done = f32[96,17]{1,0:T(8,128)} async-done(((f32[768,17]{1,0:T(8,128)}), f32[96,17]{1,0:T(8,128)}) %reduce-scatter.21.cloned.1.call-update) | async-done | bytes 6544
  1328.7 10.5 psum.62
  1339.8 75.1 %all-reduce.4.cloned.1.call-done = (f32[3,96,768]{2,1,0:T(8,128)}, f32[96,2304]{1,0:T(8,128)}, f32[96,3072]{1,0:T(8,128)}, f32[384,768]{1,0:T(8,128)}) async-done(((f32[3,96,768]{2,1,0:T(8,128)}, f32[96,2304]{1,0:T(8,128)}, f32[96,3072]{1,0:T(8,128)}, f32[384,768]{1,0:T(8,128)}), (f32[3,96,768]{2,1,0:T(8,128)}, f32[96,2304]{1,0:T(8,128)}, f32[96,3072]{1,0:T(8,128)}, ...) | async-done | bytes 4128784 | tf_op jit(solution)/shard_map/psum | solution.py:319
  1424.3 21.9 %psum.63 = f32[]{:T(128)} all-reduce(f32[]{:T(128)S(6)} %add.426), channel_id=1, replica_groups=mesh['batch'=8,'mlp'=4] {'batch'}, use_global_device_ids=true, to_apply=%region_58.59 | all-reduce | flops 1 | bytes 8 | tf_op jit(solution)/shard_map/psum | solution.py:320
  (299 shorter events, 163.7 us)
Async XLA Ops:
  7.2 43.5 %copy-start = (bf16[768,2304]{1,0:T(8,128)(2,1)S(1)}, bf16[768,2304]{1,0:T(8,128)(2,1)}, u32[]{:S(2)}) copy-start(bf16[768,2304]{1,0:T(8,128)(2,1)} %param.40) | copy-start | bytes 10616836
  7.2 113.6 %all-gather.15.cloned.1.call-start = ((), (), s32[]{:S(2)}) async-start(), calls=%async_computation.10 | async-start | bytes 6021120 | tf_op jit(solution)/shard_map/all_gather | solution.py:132
  70.1 5.5 copy-start.66
  70.1 5.7 copy-start.69
  81.8 107.1 %all-gather.7.cloned.1.call-start = ((), (), s32[]{:S(2)}) async-start(), calls=%async_computation.6 | async-start | bytes 3981312 | tf_op jit(solution)/shard_map/all_gather | solution.py:298
  82.7 172.6 %all-gather.9.cloned.1.call-start = ((), (), s32[]{:S(2)}) async-start(), calls=%async_computation.7 | async-start | bytes 3981312 | tf_op jit(solution)/shard_map/all_gather | solution.py:299
  84.9 251.5 %all-gather.11.cloned.1.call-start = ((), (), s32[]{:S(2)}) async-start(), calls=%async_computation.8 | async-start | bytes 5308416 | tf_op jit(solution)/shard_map/all_gather | solution.py:300
  85.8 35.0 %copy-start.71 = (bf16[768,768]{1,0:T(8,128)(2,1)S(1)}, bf16[768,768]{1,0:T(8,128)(2,1)}, u32[]{:S(2)}) copy-start(bf16[768,768]{1,0:T(8,128)(2,1)} %param.42) | copy-start | bytes 3538948
  85.9 331.2 %all-gather.13.cloned.1.call-start = ((), (), s32[]{:S(2)}) async-start(), calls=%async_computation.9 | async-start | bytes 5308416 | tf_op jit(solution)/shard_map/all_gather | solution.py:301
  86.8 410.5 %reduce-scatter.11.cloned.1.call-start = ((), (), s32[]{:S(2)}) async-start(), calls=%async_computation.11 | async-start | bytes 12042240 | tf_op jit(solution)/shard_map/reduce_scatter | solution.py:134
  152.7 646.4 %reduce-scatter.19.cloned.1.call-start = ((), (), s32[]{:S(2)}) async-start(), calls=%async_computation.15 | async-start | bytes 7962624
  191.8 69.3 %copy-start.16 = (f32[4,196,768]{2,1,0:T(8,128)}, f32[4,196,768]{2,1,0:T(8,128)S(1)}, u32[]{:S(2)}) copy-start(f32[4,196,768]{2,1,0:T(8,128)S(1)} %get-tuple-element.163) | copy-start | bytes 7225348
  191.8 63.5 %copy-start.49 = (f32[768]{0:T(1024)S(1)}, f32[768]{0:T(1024)}, u32[]{:S(2)}) copy-start(f32[768]{0:T(1024)} %get-tuple-element.100) | copy-start | bytes 9220
  191.8 63.5 %copy-start.57 = (f32[2304]{0:T(1024)S(1)}, f32[2304]{0:T(1024)}, u32[]{:S(2)}) copy-start(f32[2304]{0:T(1024)} %get-tuple-element.155) | copy-start | bytes 27652
  191.8 63.5 %copy-start.60 = (f32[768]{0:T(1024)S(1)}, f32[768]{0:T(1024)}, u32[]{:S(2)}) copy-start(f32[768]{0:T(1024)} %get-tuple-element.99) | copy-start | bytes 9220
  349.1 67.9 %copy-start.64 = (f32[768]{0:T(1024)S(1)}, f32[768]{0:T(1024)}, u32[]{:S(2)}) copy-start(f32[768]{0:T(1024)} %get-tuple-element.93) | copy-start | bytes 9220
  426.4 74.1 %copy-start.47 = (f32[768]{0:T(1024)S(1)}, f32[768]{0:T(1024)}, u32[]{:S(2)}) copy-start(f32[768]{0:T(1024)} %get-tuple-element.103) | copy-start | bytes 9220
  592.1 7.4 copy-start.5
  592.1 7.4 copy-start.20
  618.5 5.9 copy-start.3
  618.5 5.9 copy-start.7
  634.0 7.1 copy-start.18
  669.1 262.3 %reduce-scatter.13.cloned.1.call-start = ((), (), s32[]{:S(2)}) async-start(), calls=%async_computation.12 | async-start | bytes 7962624 | tf_op jit(solution)/shard_map/reduce_scatter | solution.py:314
  679.6 417.9 %reduce-scatter.15.cloned.1.call-start = ((), (), s32[]{:S(2)}) async-start(), calls=%async_computation.13 | async-start | bytes 10616832 | tf_op jit(solution)/shard_map/reduce_scatter | solution.py:315
  690.1 573.4 %reduce-scatter.17.cloned.1.call-start = ((), (), s32[]{:S(2)}) async-start(), calls=%async_computation.14 | async-start | bytes 10616832 | tf_op jit(solution)/shard_map/reduce_scatter | solution.py:316
  701.2 626.6 %reduce-scatter.21.cloned.1.call-start = ((), (), s32[]{:S(2)}) async-start(), calls=%async_computation.16 | async-start | bytes 442368
  705.8 709.2 %all-reduce.4.cloned.1.call-start = ((), (), s32[]{:S(2)}) async-start(), calls=%async_computation.17 | async-start | bytes 8257536 | tf_op jit(solution)/shard_map/psum | solution.py:319
  1263.5 183.4 %copy-start.46 = (f32[17,96]{1,0:T(8,128)S(1)}, f32[17,96]{1,0:T(8,128)}, u32[]{:S(2)}) copy-start(f32[17,96]{1,0:T(8,128)} %param.28) | copy-start | bytes 19588
  1263.5 183.4 %copy-start.58 = (f32[17,96]{1,0:T(8,128)S(1)}, f32[17,96]{1,0:T(8,128)}, u32[]{:S(2)}) copy-start(f32[17,96]{1,0:T(8,128)} %param.38) | copy-start | bytes 19588
  1263.5 183.4 %copy-start.59 = (f32[17,96]{1,0:T(8,128)S(1)}, f32[17,96]{1,0:T(8,128)}, u32[]{:S(2)}) copy-start(f32[17,96]{1,0:T(8,128)} %param.33) | copy-start | bytes 19588
  1263.6 184.0 %copy-start.32 = (f32[3,96,768]{2,1,0:T(8,128)S(1)}, f32[3,96,768]{2,1,0:T(8,128)}, u32[]{:S(2)}) copy-start(f32[3,96,768]{2,1,0:T(8,128)} %param.24) | copy-start | bytes 2654212
  1454.5 6.0 copy-start.1
  (58 other events, 160.4 us)
Sparse Core Ops, SparseCore 0:
  82.0 38.8 all-gather.14
  123.6 65.2 all-gather.6
  191.7 63.6 all-gather.8
  257.9 78.3 all-gather.10
  339.0 78.0 all-gather.12
  419.5 77.8 reduce-scatter.10
  669.2 129.9 reduce-scatter.18
  803.3 128.0 reduce-scatter.12
  935.0 162.4 reduce-scatter.14
  1100.9 162.5 reduce-scatter.16
  1267.3 60.4 reduce-scatter.20
  1330.9 84.0 all-reduce.3
where the time goes:
time: 1480 us; the launch traced here: 1470 us
  waiting for transfers between devices  996 us (67%)
  matrix products  187 us (13%)
  blocking collectives  104 us (7%)
  other arithmetic  83 us (6%)
  local copies, waits for them, and re-layouts  77.1 us (5%)
  between operations  21.4 us (1%)
    reduce_scatter x1, waiting for transfers between devices, on_device(): lax.psum_scatter(local[2], 'batch', scatter_dimension=0, tiled=True)  166 us
    reduce_scatter x1, waiting for transfers between devices, on_device(): lax.psum_scatter(local[3], 'batch', scatter_dimension=0, tiled=True)  166 us
    unnamed x14, waiting for transfers between devices  158 us
    reduce_scatter x1, waiting for transfers between devices, on_device(): lax.psum_scatter(local[1], 'batch', scatter_dimension=0, tiled=True)  130 us
    psum x1, waiting for transfers between devices, on_device(): lax.psum((shared[0], shared[1], shared[2], shared[3], shared[4]), 'mlp')  75.1 us
    dot_general x10, matrix products, product(): return jnp.dot(left, right, preferred_element_type=jnp.float32)  74.1 us
    reduce_scatter x1, waiting for transfers between devices, teacher_targets(): lax.psum_scatter(product(hidden, teacher_contract), 'mlp', scatter_dimens...  70.9 us
    all_gather x1, waiting for transfers between devices, on_device(): lax.all_gather(student_qkv.astype(jnp.bfloat16), 'batch', axis=0, tiled=T...  62.8 us
  transfers between devices with their start and end apart: 12, of which 12 were waited for; matrix products, arithmetic and copies ran while one was open for 10% of the time, Pallas kernels for 0%

commit v1 on v0

v1 whole, which is shorter than its diff:
```python
import functools

import jax
import jax.numpy as jnp
from jax import lax
from jax.experimental import pallas as pl
from jax.experimental.pallas import tpu as pltpu
from jax.sharding import PartitionSpec as P

D = 768
HEAD_DIM = 64
PAIR = 2 * HEAD_DIM
STEP = 10


norm_eps = 1e-06
inst_eps = 1e-05
clip_bound = 0.001
rate_matrix = 0.05
rate_vector = 0.5
decay_matrix = 0.05
beta_first = 0.9
beta_second = 0.999
adam_eps = 1e-08
f32 = jnp.float32
bf16 = jnp.bfloat16


def mm(left, right):
    return lax.dot_general(left, right, (((1,), (0,)), ((), ())), preferred_element_type=f32)


def mm_nt(left, right):
    return lax.dot_general(left, right, (((1,), (1,)), ((), ())), preferred_element_type=f32)


def mm_tn(left, right):
    return lax.dot_general(left, right, (((0,), (0,)), ((), ())), preferred_element_type=f32)


def normed_rows(values):
    centred = values - jnp.mean(values, axis=-1, keepdims=True)
    variance = jnp.mean(centred * centred, axis=-1, keepdims=True)
    scale = lax.rsqrt(variance + norm_eps)
    return centred * scale, scale


def norm_back(xhat, scale, gain, grads):
    scaled = grads * gain
    mean_one = jnp.mean(scaled, axis=-1, keepdims=True)
    mean_two = jnp.mean(scaled * xhat, axis=-1, keepdims=True)
    back = scale * (scaled - mean_one - xhat * mean_two)
    return back, total_rows(grads * xhat), total_rows(grads)


def copy_all(copies):
    for copy in copies:
        copy.start()
    for copy in copies:
        copy.wait()


def piece_copies(table_ref, semaphores, pieces):
    core = table_ref[0]
    copies = []
    for ref, (unit, height, row, near), lanes, target in pieces:
        width = lanes[1] - lanes[0]
        column = pl.multiple_of((core if near else 1 - core) * width, 128)
        for block in range(ref.shape[0]):
            place = 0 if unit == 0 else pl.multiple_of(table_ref[row + block] * unit, 16)
            copies.append(
                pltpu.make_async_copy(
                    ref.at[block, :, pl.ds(lanes[0], width)],
                    target.at[pl.ds(place, height), pl.ds(column, width)],
                    semaphores.at[len(copies)],
                )
            )
    return copies


def total_rows(values):
    return jnp.sum(values, axis=0, keepdims=True)


def head_masks(rows):
    lane = lax.broadcasted_iota(jnp.int32, (rows, PAIR), 1)
    return lane < HEAD_DIM


def stacked(values, low):
    zero = jnp.zeros_like(values)
    return jnp.concatenate([jnp.where(low, values, zero), jnp.where(low, zero, values)], axis=0)


def pair_probs(stack, keys, real_rows):
    scores = mm_nt(stack, keys)
    column = lax.broadcasted_iota(jnp.int32, scores.shape, 1)
    scores = jnp.where(column < real_rows, scores, -1e30)
    shifted = jnp.exp(scores - jnp.max(scores, axis=-1, keepdims=True))
    return shifted / jnp.sum(shifted, axis=-1, keepdims=True)


def attend_block(is_student, real_rows, pad_rows, x_ref, marks_ref, weights, vec_ref, outs):
    w0_ref, wj_ref, w1_ref = weights
    start_ref, mid_ref, joint_ref, act_ref = outs
    at = (lambda student, teacher: student if is_student else teacher)
    vec = lambda row: vec_ref[row : row + 1, :]
    block = x_ref.shape[0]
    start = mm(x_ref[...], w0_ref[...]) + vec(0)
    if is_student:
        start = jnp.where(marks_ref[:, :1] > 0, vec(1), start)
    start_ref[...] = start
    xhat, _ = normed_rows(start)
    normed = (xhat * vec(at(2, 1)) + vec(at(3, 2))).astype(bf16)
    if is_student:
        act_ref[:, D : 2 * D] = normed
        act_ref[:, 2 * D :] = x_ref[...]
    biases = (vec(at(4, 3)), None, vec(at(5, 4)))
    for part in range(3):
        cols = slice(part * D, (part + 1) * D)
        mixed = mm(normed, wj_ref[:, cols])
        if biases[part] is not None:
            mixed = mixed + biases[part]
        joint_ref[:, cols] = mixed.astype(bf16)
    low = head_masks(pad_rows)

    def one_pair(step, carry):
        image = step // (D // PAIR)
        col = pl.multiple_of((step % (D // PAIR)) * PAIR, PAIR)
        rows = pl.ds(pl.multiple_of(image * pad_rows, 16), pad_rows)
        queries = joint_ref[rows, pl.ds(col, PAIR)] * HEAD_DIM ** (-0.5)
        keys = joint_ref[rows, pl.ds(col + D, PAIR)]
        values = joint_ref[rows, pl.ds(col + 2 * D, PAIR)]
        probs = pair_probs(stacked(queries.astype(bf16), low), keys, real_rows).astype(bf16)
        mixed = mm(probs, values)
        act_ref[rows, pl.ds(col, PAIR)] = jnp.where(
            low, mixed[:pad_rows], mixed[pad_rows:]
        ).astype(bf16)
        return carry

    lax.fori_loop(0, (block // pad_rows) * (D // PAIR), one_pair, 0)
    attended = act_ref[:, :D]
    mid_ref[...] = start_ref[...] + mm(attended, w1_ref[...]) + vec(at(6, 5))


def clear_at_first(*refs):
    @pl.when(pl.program_id(0) == 0)
    def _():
        for ref in refs:
            ref[...] = jnp.zeros_like(ref)


def place_at_first(table_ref, semaphores, pieces):
    @pl.when(pl.program_id(0) == 0)
    def _():
        copy_all(piece_copies(table_ref, semaphores, pieces))


def attend_teacher_kernel(real_rows, pad_rows, *refs):
    (x_ref, w0_ref, wj_ref, w1_ref, vec_ref, mid_ref, joint_ref, att_ref) = refs
    attend_block(
        False,
        real_rows,
        pad_rows,
        x_ref,
        None,
        (w0_ref, wj_ref, w1_ref),
        vec_ref,
        (mid_ref, mid_ref, joint_ref, att_ref),
    )


def attend_student_kernel(real_rows, pad_rows, metas, joint_metas, *refs):
    (table_ref, x_ref, marks_ref, vec_ref) = refs[:4]
    count = len(metas)
    piece_refs, joint_refs = refs[4 : 4 + count], refs[4 + count : 4 + 2 * count]
    (start_ref, mid_ref, joint_ref, act_ref) = refs[4 + 2 * count : 8 + 2 * count]
    (w0_ref, w1_ref, wj_ref, semaphores) = refs[8 + 2 * count :]
    pieces = section(piece_refs, metas, SQUARE_LANES[0], w0_ref)
    pieces += section(joint_refs, joint_metas, JOINT_LANES, wj_ref)
    pieces += section(piece_refs, metas, SQUARE_LANES[1], w1_ref)
    place_at_first(table_ref, semaphores, pieces)
    attend_block(
        True,
        real_rows,
        pad_rows,
        x_ref,
        marks_ref,
        (w0_ref, wj_ref, w1_ref),
        vec_ref,
        (start_ref, mid_ref, joint_ref, act_ref),
    )


def gelu_half(values):
    return 0.5 * (1.0 + lax.erf(values * 0.7071067811865476))


def teacher_ffn_kernel(real_rows, pad_rows, is_last, *refs):
    mid_ref, bias_ref, vec_ref = refs[:3]
    parts = bias_ref.shape[0]
    rest = refs[3 + parts :]
    mid = mid_ref[...]
    xhat, _ = normed_rows(mid)
    normed = (xhat * vec_ref[6:7, :] + vec_ref[7:8, :]).astype(bf16)
    total = rest[0][...] if is_last else None
    for part, both_ref in enumerate(refs[3 : 3 + parts]):
        pre = mm(normed, both_ref[:, :D]) + bias_ref[part : part + 1, :]
        hidden = (pre * gelu_half(pre)).astype(bf16)
        piece = mm(hidden, both_ref[:, D:])
        total = piece if total is None else total + piece
    out_ref = rest[-1]
    if not is_last:
        out_ref[...] = total
        return
    total = total + vec_ref[12:13, :]
    valid = lax.broadcasted_iota(jnp.int32, (pad_rows, D), 0) < real_rows
    for image in range(mid_ref.shape[0] // pad_rows):
        rows = slice(image * pad_rows, (image + 1) * pad_rows)
        result = None
        for values in (mid[rows], total[rows]):
            mean = total_rows(jnp.where(valid, values, 0.0)) / real_rows
            centred = values - mean
            variance = total_rows(jnp.where(valid, centred * centred, 0.0)) / real_rows
            normal = centred * lax.rsqrt(variance + inst_eps)
            result = normal if result is None else result + normal
        out_ref[rows, :] = 0.5 * result


def student_ffn_kernel(square_metas, expand_metas, contract_metas, *refs):
    (table_ref, scale_ref, mid_ref, target_ref, marks_ref, vec_ref) = refs[:6]
    counts = (len(square_metas), len(expand_metas), len(contract_metas))
    square_refs = refs[6 : 6 + counts[0]]
    expand_refs = refs[6 + counts[0] : 6 + counts[0] + counts[1]]
    contract_refs = refs[6 + counts[0] + counts[1] : 6 + sum(counts)]
    (keep_ref, one_ref, two_ref, dmid_ref, sum_ref) = refs[6 + sum(counts) : 11 + sum(counts)]
    (we_ref, wc_ref, wh_ref, slope_ref, half_ref, semaphores) = refs[11 + sum(counts) :]
    pieces = section(expand_refs, expand_metas, (0, 2 * D), we_ref)
    pieces += section(contract_refs, contract_metas, (0, D // 2), wc_ref)
    pieces += section(square_refs, square_metas, SQUARE_LANES[2], wh_ref)
    clear_at_first(sum_ref)
    place_at_first(table_ref, semaphores, pieces)
    core = table_ref[0]

    def add(row, values):
        sum_ref[pl.ds(row, 1), :] += values

    def add_grad(row, grads):
        add(row, total_rows(grads.astype(f32)))

    def halves(keep_cols, send_ref, send_cols, grads):
        half_ref[...] = grads
        width = D // 2
        keep_ref[:, keep_cols : keep_cols + width] = half_ref[
            :, pl.ds(pl.multiple_of(core * width, 128), width)
        ]
        send_ref[:, send_cols : send_cols + width] = half_ref[
            :, pl.ds(pl.multiple_of((1 - core) * width, 128), width)
        ]

    vec = lambda row: vec_ref[row : row + 1, :]
    mid = mid_ref[...]
    xhat2, scale2 = normed_rows(mid)
    n2 = (xhat2 * vec(7) + vec(8)).astype(bf16)
    one_ref[:, D : 2 * D] = n2
    total = None
    for part in range(4):
        cols = slice(part * D, (part + 1) * D)
        pre = mm(n2, we_ref[:, cols]) + vec(9 + part)
        half = gelu_half(pre)
        slope_ref[:, cols] = half + pre * (jnp.exp(-0.5 * pre * pre) * 0.3989422804014327)
        hidden = (pre * half).astype(bf16)
        two_ref[:, cols] = hidden
        piece = mm(hidden, wc_ref[cols, :])
        total = piece if total is None else total + piece
    final = mid + total + vec(13)
    xhat3, scale3 = normed_rows(final)
    n3 = (xhat3 * vec(14) + vec(15)).astype(bf16)
    one_ref[:, :D] = n3
    error = marks_ref[:, :1] * (mm(n3, wh_ref[...]) + vec(16) - target_ref[...])
    add(0, total_rows(error * error))
    dpred = (error * scale_ref[0]).astype(bf16)
    halves(2 * D, one_ref, 4 * D, dpred)
    add_grad(1, dpred)
    dfinal, gain3, shift3 = norm_back(xhat3, scale3, vec(14), mm_nt(dpred, wh_ref[...]))
    add(2, gain3)
    add(3, shift3)
    dbranch = dfinal.astype(bf16)
    halves(2 * D + D // 2, two_ref, 4 * D, dbranch)
    add_grad(4, dbranch)
    dn2 = None
    for side in range(2):
        for part in range(2):
            chunk = 2 * (core ^ side) + part
            cols = pl.ds(pl.multiple_of(chunk * D, 128), D)
            dpre = (mm_nt(dbranch, wc_ref[cols, :]) * slope_ref[:, cols]).astype(bf16)
            if side == 0:
                keep_ref[:, part * D : (part + 1) * D] = dpre
            else:
                one_ref[:, (2 + part) * D : (3 + part) * D] = dpre
            add_grad(5 + chunk, dpre)
            piece = mm_nt(dpre, we_ref[:, cols])
            dn2 = piece if dn2 is None else dn2 + piece
    dmid, gain2, shift2 = norm_back(xhat2, scale2, vec(7), dn2)
    add(9, gain2)
    add(10, shift2)
    dmid = dfinal + dmid
    dmid_ref[...] = dmid
    add(11, total_rows(dmid.astype(bf16).astype(f32)))


def attend_back_kernel(real_rows, pad_rows, metas, joint_metas, *refs):
    (table_ref, dmid_ref, joint_ref, start_ref, marks_ref, vec_ref) = refs[:6]
    count = len(metas)
    piece_refs, joint_refs = refs[6 : 6 + count], refs[6 + count : 6 + 2 * count]
    (keep_ref, send_ref, sum_ref) = refs[6 + 2 * count : 9 + 2 * count]
    (w1_ref, wj_ref, grad_ref, djoint_ref, half_ref, semaphores) = refs[9 + 2 * count :]
    pieces = section(piece_refs, metas, SQUARE_LANES[1], w1_ref)
    pieces += section(joint_refs, joint_metas, JOINT_LANES, wj_ref)
    clear_at_first(sum_ref)
    place_at_first(table_ref, semaphores, pieces)
    core = table_ref[0]

    def add(row, values):
        sum_ref[row : row + 1, :] += values

    def halves(column, source_ref, width):
        keep_ref[:, column : column + width] = source_ref[
            :, pl.ds(pl.multiple_of(core * width, 128), width)
        ]
        send_ref[:, column : column + width] = source_ref[
            :, pl.ds(pl.multiple_of((1 - core) * width, 128), width)
        ]

    vec = lambda row: vec_ref[row : row + 1, :]
    block = dmid_ref.shape[0]
    datt = dmid_ref[...].astype(bf16)
    half_ref[...] = datt
    halves(0, half_ref, D // 2)
    grad_ref[...] = mm_nt(datt, w1_ref[...]).astype(bf16)
    low = head_masks(pad_rows)

    def one_pair(step, carry):
        image = step // (D // PAIR)
        col = pl.multiple_of((step % (D // PAIR)) * PAIR, PAIR)
        rows = pl.ds(pl.multiple_of(image * pad_rows, 16), pad_rows)
        queries = joint_ref[rows, pl.ds(col, PAIR)] * HEAD_DIM ** (-0.5)
        keys = joint_ref[rows, pl.ds(col + D, PAIR)]
        values = joint_ref[rows, pl.ds(col + 2 * D, PAIR)]
        stack = stacked(queries.astype(bf16), low)
        dstack = stacked(grad_ref[rows, pl.ds(col, PAIR)], low)
        probs = pair_probs(stack, keys, real_rows)
        dprobs = mm_nt(dstack, values)
        dvalues = mm_tn(probs.astype(bf16), dstack)
        weighted = probs * dprobs
        dscores = (weighted - probs * jnp.sum(weighted, axis=-1, keepdims=True)).astype(bf16)
        both = mm(dscores, keys) * HEAD_DIM ** (-0.5)
        dqueries = jnp.where(low, both[:pad_rows], both[pad_rows:])
        dkeys = mm_tn(dscores, stack)
        djoint_ref[rows, pl.ds(col, PAIR)] = dqueries.astype(bf16)
        djoint_ref[rows, pl.ds(col + D, PAIR)] = dkeys.astype(bf16)
        djoint_ref[rows, pl.ds(col + 2 * D, PAIR)] = dvalues.astype(bf16)
        return carry

    lax.fori_loop(0, (block // pad_rows) * (D // PAIR), one_pair, 0)
    halves(D // 2, djoint_ref, 3 * D // 2)
    dnormed = None
    for part in range(3):
        cols = slice(part * D, (part + 1) * D)
        grads = djoint_ref[:, cols]
        if part != 1:
            add(part // 2, total_rows(grads.astype(f32)))
        piece = mm_nt(grads, wj_ref[:, cols])
        dnormed = piece if dnormed is None else dnormed + piece
    xhat, scale = normed_rows(start_ref[...])
    dstart, gain, shift = norm_back(xhat, scale, vec(2), dnormed)
    add(2, gain)
    add(3, shift)
    dstart = dstart + dmid_ref[...]
    masked = marks_ref[:, :1] > 0
    add(4, total_rows(jnp.where(masked, dstart, 0.0)))
    dembed = jnp.where(masked, 0.0, dstart).astype(bf16)
    half_ref[...] = dembed
    halves(2 * D, half_ref, D // 2)
    add(5, total_rows(dembed.astype(f32)))


def store_members(out_ref, table_ref, result, members, relative_y):
    rows = result.shape[0] // members
    for member in range(members):
        place = member ^ table_ref[2]
        for side in range(2):
            first = member * rows + side * (rows // 2)
            target = (side ^ table_ref[1]) if relative_y else side
            out_ref[place, target] = result[first : first + rows // 2]


def weight_grad_kernel(members, relative, relative_y, is_new, *refs):
    (table_ref, a_ref, a_peer_ref, b_ref, b_peer_ref, out_ref, top_ref, turned_ref) = refs

    @pl.when(is_new(pl.program_id(0)))
    def _():
        turned_ref[0] = a_ref[...].T
        turned_ref[1] = a_peer_ref[...].T

    result = mm(turned_ref[0], b_ref[...]) + mm(turned_ref[1], b_peer_ref[...])
    top_ref[...] = jnp.broadcast_to(jnp.max(jnp.abs(result), axis=0, keepdims=True), top_ref.shape)
    if relative:
        store_members(out_ref, table_ref, result, members, relative_y)
    else:
        out_ref[...] = result


def contract_grad_kernel(relative, *refs):
    (table_ref, d_ref, d_peer_ref, h_ref, h_peer_ref, out_ref, top_ref, turned_ref) = refs
    clear_at_first(top_ref)

    @pl.when(pl.program_id(0) == 0)
    def _():
        turned_ref[0] = d_ref[...].T
        turned_ref[1] = d_peer_ref[...].T

    result = (mm(turned_ref[0], h_ref[...]) + mm(turned_ref[1], h_peer_ref[...])).T
    top_ref[...] = jnp.maximum(top_ref[...], jnp.max(jnp.abs(result), axis=0, keepdims=True))
    if relative:
        rows = result.shape[0] // 2
        for side in range(2):
            out_ref[0, side ^ table_ref[1]] = result[side * rows : (side + 1) * rows]
    else:
        out_ref[...] = result


SQUARE_LANES = tuple((i * D // 2, (i + 1) * D // 2) for i in range(3))
JOINT_LANES = (0, 3 * D // 2)


def section(refs, metas, lanes, target):
    return [(ref, meta, lanes, target) for ref, meta in zip(refs, metas)]


def blocks_of(group):
    return sum(array.shape[0] for array in group[0])


def whole_spec(shape):
    return pl.BlockSpec(shape, lambda *_: (0,) * len(shape), pipeline_mode=pl.Buffered(1))


def row_spec(block, width):
    return pl.BlockSpec((block, width), lambda i, *_: (i, 0))


COSTS = {'attend_teacher': 13.0, 'attend_student': 29.0, 'teacher_ffn': 9.0, 'student_ffn': 35.0, 'attend_back': 36.0, 'grad_expand': 15.0, 'grad_contract': 13.0, 'grad_out_joint': 9.0, 'grad_joint_embed': 11.0}
smem_spec = pl.BlockSpec(memory_space=pltpu.SMEM)
any_spec = pl.BlockSpec(memory_space=pl.ANY)


def call(kernel, name, grid, ins, outs, scratch, flops, moved, prefetch=0):
    return pl.pallas_call(
        kernel,
        grid_spec=pltpu.PrefetchScalarGridSpec(
            num_scalar_prefetch=prefetch,
            grid=grid,
            in_specs=[spec for _, spec in ins[prefetch:]],
            out_specs=[spec for _, spec in outs],
            scratch_shapes=scratch,
        ),
        out_shape=[jax.ShapeDtypeStruct(*item) for item, _ in outs],
        compiler_params=pltpu.CompilerParams(vmem_limit_bytes=60 << 20),
        cost_estimate=pl.CostEstimate(
            flops=int(COSTS[name] * 1.15e9), transcendentals=0, bytes_accessed=1
        ),
        name=name,
    )(*[item for item, _ in ins])


def attend_teacher(real_rows, pad_rows, images, first, x, w0, wj, w1, vectors):
    rows = block = images * pad_rows
    wholes = [(item, whole_spec(item.shape)) for item in (w0, wj, w1, vectors)]
    return call(
        functools.partial(attend_teacher_kernel, real_rows, pad_rows),
        "attend_teacher",
        (rows // block,),
        [(x, pl.BlockSpec((block, D), lambda i, *_: (first, 0)))] + wholes,
        [(((rows, D), f32), row_spec(block, D))],
        [pltpu.VMEM((block, 3 * D), bf16), pltpu.VMEM((block, D), bf16)],
        14 * rows * D * D,
        20e6,
    )[0]


def attend_student(real_rows, pad_rows, images, table, x, marks, vectors, square, joint):
    rows, block = x.shape[0], images * pad_rows
    arrays, metas = square[0] + joint[0], (square[1], joint[1])
    outs = [(D, f32), (D, f32), (3 * D, bf16), (3 * D, bf16)]
    return call(
        functools.partial(attend_student_kernel, real_rows, pad_rows, *metas),
        "attend_student",
        (rows // block,),
        [
            (table, smem_spec),
            (x, row_spec(block, D)),
            (marks, row_spec(block, 128)),
            (vectors, whole_spec(vectors.shape)),
        ]
        + [(array, any_spec) for array in arrays],
        [(((rows, width), kind), row_spec(block, width)) for width, kind in outs],
        [
            pltpu.VMEM((D, D), bf16),
            pltpu.VMEM((D, D), bf16),
            pltpu.VMEM((D, 3 * D), bf16),
            pltpu.SemaphoreType.DMA((2 * blocks_of(square) + blocks_of(joint),)),
        ],
        14 * rows * D * D,
        25e6,
    )


def teacher_ffn(real_rows, pad_rows, images, mid, weights, biases, vectors, sums):
    rows, block = mid.shape[0], images * pad_rows
    items = [biases, vectors, *weights]
    wholes = [(item, whole_spec(item.shape)) for item in items]
    last = [] if sums is None else [(sums, row_spec(block, D))]
    return call(
        functools.partial(teacher_ffn_kernel, real_rows, pad_rows, sums is not None),
        "teacher_ffn",
        (rows // block,),
        [(mid, row_spec(block, D))] + wholes + last,
        [(((rows, D), f32), row_spec(block, D))],
        [],
        16 * rows * D * D,
        15e6,
    )[0]


def student_ffn(pad_rows, images, table, scale, mid, targets, marks, vectors, square, expand, contract):
    rows, block = mid.shape[0], images * pad_rows
    outs = [(3 * D, bf16), (9 * D // 2, bf16), (9 * D // 2, bf16), (D, f32)]
    return call(
        functools.partial(student_ffn_kernel, square[1], expand[1], contract[1]),
        "student_ffn",
        (rows // block,),
        [
            (table, smem_spec),
            (scale, smem_spec),
            (mid, row_spec(block, D)),
            (targets, row_spec(block, D)),
            (marks, row_spec(block, 128)),
            (vectors, whole_spec(vectors.shape)),
        ]
        + [(array, any_spec) for array in (*square[0], *expand[0], *contract[0])],
        [(((rows, width), kind), row_spec(block, width)) for width, kind in outs]
        + [(((16, D), f32), whole_spec((16, D)))],
        [
            pltpu.VMEM((D, 4 * D), bf16),
            pltpu.VMEM((4 * D, D), bf16),
            pltpu.VMEM((D, D), bf16),
            pltpu.VMEM((block, 4 * D), f32),
            pltpu.VMEM((block, D), bf16),
            pltpu.SemaphoreType.DMA((blocks_of(square) + blocks_of(expand) + blocks_of(contract),)),
        ],
        36 * rows * D * D,
        40e6,
    )


def attend_back(
    real_rows, pad_rows, images, table, dmid, joint, start, marks, vectors, square, qkv
):
    rows, block = dmid.shape[0], images * pad_rows
    arrays, metas = square[0] + qkv[0], (square[1], qkv[1])
    return call(
        functools.partial(attend_back_kernel, real_rows, pad_rows, *metas),
        "attend_back",
        (rows // block,),
        [
            (table, smem_spec),
            (dmid, row_spec(block, D)),
            (joint, row_spec(block, 3 * D)),
            (start, row_spec(block, D)),
            (marks, row_spec(block, 128)),
            (vectors, whole_spec(vectors.shape)),
        ]
        + [(array, any_spec) for array in arrays],
        [(((rows, 5 * D // 2), bf16), row_spec(block, 5 * D // 2))] * 2
        + [(((16, D), f32), whole_spec((16, D)))],
        [
            pltpu.VMEM((D, D), bf16),
            pltpu.VMEM((D, 3 * D), bf16),
            pltpu.VMEM((block, D), bf16),
            pltpu.VMEM((block, 3 * D), bf16),
            pltpu.VMEM((block, D), bf16),
            pltpu.SemaphoreType.DMA((blocks_of(square) + blocks_of(qkv),)),
        ],
        20 * rows * D * D,
        25e6,
    )


def relative_rows(grads, members, relative_y, place, own_y):
    grads = grads.reshape(members, 2, -1, grads.shape[1])
    grads = jnp.take(grads, jnp.arange(members) ^ place, axis=0)
    if relative_y:
        grads = jnp.take(grads, jnp.arange(2) ^ own_y, axis=1)
    return grads


def weight_grad(name, table, members, relative_y, steps, own_a, peer_a, own_b, peer_b, is_new):
    rows = own_a[0].shape[0]
    wide = D // 2
    relative = (D // members) % 16 == 0

    def spec(item):
        return (item[0], pl.BlockSpec((rows, item[1]), lambda j, _: (0, item[2](j))))

    if relative:
        shape = (members, 2, D // members // 2)
        out = ((shape + (steps * wide,), f32), pl.BlockSpec(shape + (wide,), lambda j, _: (0, 0, 0, j)))
    else:
        out = (((D, steps * wide), f32), pl.BlockSpec((D, wide), lambda j, _: (0, j)))
    grads, top = call(
        functools.partial(weight_grad_kernel, members, relative, relative_y, is_new),
        name,
        (steps,),
        [(table, None), spec(own_a), spec(peer_a), spec(own_b), spec(peer_b)],
        [out, (((8, steps * wide), f32), pl.BlockSpec((8, wide), lambda j, _: (0, j)))],
        [pltpu.VMEM((2, D, rows), bf16)],
        4 * rows * D * wide * steps,
        4 * D * wide * steps + 4 * rows * (D + wide * steps),
        prefetch=1,
    )
    if not relative:
        grads = relative_rows(grads, members, relative_y, table[2], table[1])
    return grads, top[:1]


def contract_grad(table, members, keep, own, peer):
    rows = own.shape[0]
    wide = D // 2
    height = 4 * D // members
    relative = height == wide
    column = lambda index: pl.BlockSpec((rows, wide), lambda i, _: (0, index))
    moving = pl.BlockSpec((rows, wide), lambda i, _: (0, i))
    if relative:
        out = (
            ((members, 2, height // 2, wide), f32),
            pl.BlockSpec((1, 2, height // 2, wide), lambda i, t: (i ^ t[2], 0, 0, 0)),
        )
    else:
        out = (((4 * D, wide), f32), pl.BlockSpec((wide, wide), lambda i, _: (i, 0)))
    grads, top = call(
        functools.partial(contract_grad_kernel, relative),
        "grad_contract",
        (4 * D // wide,),
        [(table, None), (keep, column(5)), (peer, column(8)), (own, moving), (peer, moving)],
        [out, (((8, wide), f32), whole_spec((8, wide)))],
        [pltpu.VMEM((2, wide, rows), bf16)],
        16 * rows * D * wide,
        16 * D * wide + 16 * rows * D,
        prefetch=1,
    )
    if not relative:
        grads = relative_rows(grads, members, True, table[2], table[1])
    return grads, top[:1]


def after(value, *others):
    return lax.optimization_barrier((value, *others))[0]


def swap(values, bit):
    total = lax.axis_size("batch") * lax.axis_size("mlp")
    return lax.ppermute(values, ("batch", "mlp"), [(i, i ^ bit) for i in range(total)])


def batch_swap(values, bit):
    return swap(values, lax.axis_size("mlp") << bit)


def bit_of(axis, bit):
    return (lax.axis_index(axis) >> bit) & 1


def all_sum(values, bits):
    for bit in bits:
        values = values + swap(values, 1 << bit)
    return values


def half_of(values, which, axis):
    width = values.shape[axis] // 2
    return lax.dynamic_slice_in_dim(values, which * width, width, axis)


def in_order(first, second, bit_value, axis):
    return jnp.where(
        bit_value == 0,
        jnp.concatenate([first, second], axis),
        jnp.concatenate([second, first], axis),
    )


def natural_rows(blocks, order):
    count = len(order)
    full = blocks.reshape((2,) * count + blocks.shape[1:])
    for place in range(count):
        flip = bit_of("batch", order[count - 1 - place])
        full = jnp.where(flip == 0, full, jnp.flip(full, place))
    source = [count - 1 - order.index(bit) for bit in reversed(range(count))]
    full = full.transpose(source + [count, count + 1])
    return full.reshape(1, -1, full.shape[-1])


def blocks_group(held, last, order, row):
    members = 1 << len(order)
    height = held.shape[1]
    if height % 16 != 0:
        return whole_group(natural_rows(jnp.concatenate([held, last], 0), order), row)
    entries = [
        lax.axis_index("batch") ^ sum(((p >> j) & 1) << bit for j, bit in enumerate(order))
        for p in range(members)
    ]
    arrays = [held, last, swap(held, 1), swap(last, 1)]
    metas = [
        (height, height, row + part * (members // 2), near)
        for near in (True, False)
        for part in (0, 1)
    ]
    return (arrays, tuple(metas)), entries


def whole_group(near, row):
    metas = tuple((0, near.shape[1], row, side) for side in (True, False))
    return ([near, swap(near, 1)], metas), []


def power_of_two(exponent):
    size = jnp.abs(exponent).astype(jnp.int32)
    result = jnp.ones_like(exponent)
    for bit in range(7):
        factor = jnp.where(exponent > 0, 2.0 ** (1 << bit) if bit < 7 else 1.0, 2.0 ** -(1 << bit))
        result = jnp.where((size >> bit) & 1 == 1, result * factor, result)
    return result


def packed(values, bound):
    exponent = jnp.floor(14.0 - jnp.log2(jnp.clip(bound, 1e-30, 1e30)))
    scaled = lax.reduce_precision(values * power_of_two(exponent), 5, 10).astype(jnp.float16)
    tail = jnp.broadcast_to(exponent.astype(jnp.float16), (16, exponent.shape[1]))
    return jnp.concatenate([scaled.reshape(-1, scaled.shape[-1]), tail], 0)


def unpacked(rows, shape):
    exponent = rows[-1:].astype(f32)
    values = rows[:-16].astype(f32) * power_of_two(-exponent)
    return values.reshape(shape), power_of_two(15.0 - exponent)


def first_axis_half(sums, place):
    return lax.index_in_dim(sums, 0, place, keepdims=False), lax.index_in_dim(
        sums, 1, place, keepdims=False
    )


class Reduction:
    def __init__(self, blocks, top, order, y_first):
        count = len(order)
        self.sums = blocks.reshape((2,) * count + blocks.shape[1:])
        self.bound = top
        self.left = list(reversed(range(count))) + ["y"]
        self.hops = (["y"] if y_first else []) + list(order)
        self.y_first = y_first
        self.sent = None

    def send(self, *gates):
        if self.hops:
            place = self.left.index(self.hops[0])
            self.left.remove(self.hops[0])
            self.sums, sent = first_axis_half(self.sums, place)
            self.sent = packed(after(sent, *gates), self.bound)
        else:
            self.sent = packed(after(self.sums, *gates), self.bound)
        return self.sent

    def receive(self):
        if not self.hops:
            other = swap(self.sent, 2)
            own, _ = unpacked(self.sent, self.sums.shape)
            other, _ = unpacked(other, self.sums.shape)
            if self.y_first:
                self.sums = in_order(own, other, bit_of("mlp", 1), 0)
            else:
                self.sums = (own + other).reshape(-1, own.shape[-1])
            return self
        bit = self.hops.pop(0)
        other = swap(self.sent, 2) if bit == "y" else batch_swap(self.sent, bit)
        other, bound = unpacked(other, self.sums.shape)
        self.sums = self.sums + other
        self.bound = self.bound + bound
        return self

    def hop(self, *gates):
        self.send(*gates)
        return self.receive()

    def finish(self):
        while self.hops:
            self.hop()
        return self.hop().sums


def adam_update(master, first, second, gradient, step_rate, weight_decay):
    moment = beta_first * first + (1.0 - beta_first) * gradient
    variance = beta_second * second + (1.0 - beta_second) * gradient * gradient
    corrected = moment / (1.0 - beta_first**STEP)
    scaled = variance / (1.0 - beta_second**STEP)
    updated = master - step_rate * (
        corrected / (jnp.sqrt(scaled) + adam_eps) + weight_decay * master
    )
    return (moment, variance, updated)


def on_device(
    patches,
    mask,
    student_square,
    student_qkv,
    student_expand,
    student_contract,
    student_vectors,
    first_square,
    first_qkv,
    first_expand,
    first_contract,
    first_vectors,
    second_square,
    second_qkv,
    second_expand,
    second_contract,
    second_vectors,
    teacher_square,
    teacher_qkv,
    teacher_expand,
    teacher_contract,
    teacher_vectors,
):
    members = lax.axis_size("batch")
    count = members.bit_length() - 1
    mlp_bits = lax.axis_size("mlp").bit_length() - 1
    near = list(range(count))
    far = near[::-1]
    batch_bits = range(mlp_bits, mlp_bits + count)
    shard_rows = D // members
    core, own_y = bit_of("mlp", 0), bit_of("mlp", 1)
    place = lax.axis_index("batch")
    group, real_rows = mask.shape
    pad_rows = -(-real_rows // 16) * 16
    half = D // 2

    pad = ((0, 0), (0, pad_rows - real_rows))
    x = jnp.pad(patches, pad + ((0, 0),)).reshape(-1, D)
    marks = jnp.pad(mask.astype(f32), pad).reshape(-1)
    wide_marks = jnp.broadcast_to(marks[:, None], (marks.shape[0], 128))

    square_half = jnp.concatenate([half_of(student_square[i], core, 1) for i in range(3)], 1)
    square_held = square_half.astype(bf16)[None]
    qkv_held = half_of(student_qkv, core, 1).astype(bf16)[None]
    expand_near = lax.all_gather(
        half_of(student_expand, core, 1).astype(bf16), "batch", axis=0, tiled=True
    )
    contract_near = lax.all_gather(
        half_of(student_contract, core, 1).astype(bf16), "batch", axis=0, tiled=True
    )
    teacher_own = jnp.concatenate([teacher_expand, teacher_contract], 1)
    teacher_y = swap(teacher_own, 2)
    teacher_core = swap(teacher_own, 1)
    low_vectors = lax.reduce_precision(student_vectors, 8, 7)
    small = lax.dynamic_update_slice(
        jnp.zeros((low_vectors.shape[0], D), f32), low_vectors, (0, place * shard_rows)
    )
    small = jnp.concatenate([small, jnp.full((1, D), jnp.sum(marks))], 0)

    images = min(group, 2)
    sizes = (real_rows, pad_rows, images)
    teacher_weights = (teacher_square[0], teacher_qkv, teacher_square[1], teacher_vectors)
    own = lax.axis_index("mlp")
    biases = jnp.concatenate(
        [lax.dynamic_slice_in_dim(teacher_vectors, 8 + (own ^ part), 1, 0) for part in range(4)]
    )
    tmids, tsum, done = [], None, ()
    square_order, qkv_order = far, near[:1] + far[:-1]
    for hop in range(count):
        sends = lax.optimization_barrier((square_held, qkv_held, small, *done))[:3]
        square_held, qkv_held, small = sends
        square_last = batch_swap(square_held, square_order[hop])
        qkv_last = batch_swap(qkv_held, qkv_order[hop])
        small_last = batch_swap(small, near[hop])
        if len(tmids) < group // images:
            item = attend_teacher(*sizes, len(tmids), after(x, *sends), *teacher_weights)
            tmids.append(item)
            done = (item,)
        elif tsum is None:
            tmid = jnp.concatenate(tmids, 0)
            tsum = teacher_ffn(
                *sizes,
                after(tmid, *sends),
                (teacher_own, teacher_core),
                biases[:2],
                teacher_vectors,
                None,
            )
            done = (tsum,)
        if hop + 1 < count:
            square_held = jnp.concatenate([square_held, square_last], 0)
            qkv_held = jnp.concatenate([qkv_held, qkv_last], 0)
        small = small + small_last
    vectors = small[:-1]
    square_held, qkv_held, square_last, qkv_last = lax.optimization_barrier(
        (square_held, qkv_held, square_last, qkv_last, *done)
    )[:4]
    square, square_rows = blocks_group(square_held, square_last, square_order, 3)
    qkv, qkv_rows = blocks_group(qkv_held, qkv_last, qkv_order, 3 + len(square_rows))
    entries = [core, own_y, place] + square_rows + qkv_rows
    table = jnp.stack([jnp.asarray(entry, jnp.int32) for entry in entries])

    masked_count = all_sum(small[-1:, :128], range(mlp_bits))[0, 0]
    teacher_far = swap(after(teacher_y, small), 1)
    start, mid, joint, act = attend_student(
        *sizes, table, after(x, tsum), wide_marks, vectors, square, qkv
    )
    act_peer = swap(act, 1)
    expand, _ = whole_group(after(expand_near, mid)[None], 0)
    contract, _ = whole_group(after(contract_near, mid)[None], 0)
    targets = teacher_ffn(
        *sizes,
        after(tmid, mid),
        (teacher_y, teacher_far),
        biases[2:],
        teacher_vectors,
        tsum,
    )
    scale = (2.0 / (masked_count * D)).reshape(1)
    keep, one, two, dmid, ffn_sums = student_ffn(
        pad_rows, images, table, scale, mid, targets, wide_marks, vectors, square, expand, contract
    )
    one_peer, two_peer = swap(one, 1), swap(two, 1)

    blocks, top = weight_grad(
        "grad_expand",
        table,
        members,
        False,
        5,
        (one, D, lambda j: 1 - j // 4),
        (one_peer, D, lambda j: 1 - j // 4),
        (keep, half, lambda j: j),
        (one_peer, half, lambda j: j + 4),
        lambda j: (j == 0) | (j == 4),
    )
    to_expand = Reduction(blocks, top, near, False)
    sent = to_expand.send()
    blocks, top = contract_grad(table, members, keep, two, after(two_peer, sent))
    to_contract = Reduction(blocks, top, near, True)
    sent = to_contract.send()
    keep3, send3, att_sums = attend_back(
        *sizes, table, after(dmid, sent), joint, start, wide_marks, vectors, square, qkv
    )
    total = jnp.concatenate([ffn_sums[:12], att_sums[:6]], 0)
    total_bits = list(range(mlp_bits + count))
    send3_peer = swap(send3, 1)
    moving = [to_expand, to_contract]

    def receive_all():
        for item in moving:
            item.receive()

    def send_all(*gates):
        return [item.send(*gates) for item in moving]

    def total_hop(*gates):
        nonlocal total
        if total_bits:
            total = after(total, *gates)
            total = total + swap(total, 1 << total_bits.pop(0))

    receive_all()
    sent = send_all(keep3)
    blocks, top = weight_grad(
        "grad_out_joint",
        table,
        members,
        False,
        2,
        (act, D, lambda j: j),
        (act_peer, D, lambda j: j),
        (keep3, half, lambda j: j),
        (after(send3_peer, *sent), half, lambda j: j),
        lambda j: j >= 0,
    )
    total_hop(*sent)
    receive_all()
    to_first = Reduction(blocks, top, near, False)
    moving.append(to_first)
    sent = send_all(blocks)
    blocks, top = weight_grad(
        "grad_joint_embed",
        table,
        members,
        True,
        3,
        (act, D, lambda j: 1 + j // 2),
        (act_peer, D, lambda j: 1 + j // 2),
        (keep3, half, lambda j: j + 2),
        (after(send3_peer, total, *sent), half, lambda j: j + 2),
        lambda j: (j == 0) | (j == 2),
    )
    total_hop(*sent)
    receive_all()
    to_second = Reduction(blocks, top, near, True)
    moving.append(to_second)
    gates = (blocks,)
    while moving:
        total_hop(*send_all(*gates))
        for item in list(moving):
            is_last = not item.hops
            item.receive()
            if is_last:
                moving.remove(item)
        gates = ()
    while total_bits:
        total_hop()
    sum_expand, sum_contract = to_expand.sums, to_contract.sums
    sum_first, sum_second = to_first.sums, to_second.sums
    ffn_total, att_total = total[:12], total[12:]

    own_sums = (sum_expand, sum_contract, sum_first, sum_second)
    vector_total = jnp.concatenate(
        [
            att_total[5:6],
            att_total[4:5],
            att_total[2:4],
            att_total[0:2],
            ffn_total[11:12],
            ffn_total[9:11],
            ffn_total[5:9],
            ffn_total[4:5],
            ffn_total[2:4],
            ffn_total[1:2],
        ]
    )
    loss_sum = jnp.sum(ffn_total[0])
    vector_grad = lax.dynamic_slice_in_dim(vector_total, place * shard_rows, shard_rows, 1)
    squares = 0.5 * jnp.sum(vector_grad * vector_grad)
    for member in own_sums:
        squares = squares + jnp.sum(member * member)
    squares = all_sum(jnp.full((1, 128), squares), [0, *batch_bits])
    grad_norm = jnp.sqrt(squares[0, 0])
    factor = clip_bound / jnp.maximum(grad_norm, clip_bound)

    pairs = [(item, swap(item, 1)) for item in own_sums]

    def columns(index, first, last):
        return [item[:, first:last] for item in pairs[index]]

    joint_pair = [
        jnp.concatenate([left, right], 1)
        for left, right in zip(columns(2, half, 2 * half), columns(3, 0, 2 * half))
    ]
    whole = lambda pair: in_order(pair[0], pair[1], core, 1)
    grads = (
        jnp.stack(
            [
                whole(columns(3, 2 * half, 3 * half)),
                whole(columns(2, 0, half)),
                whole(columns(0, 4 * half, 5 * half)),
            ]
        ),
        whole(joint_pair),
        whole(columns(0, 0, 4 * half)),
        whole(columns(1, 0, half)),
        vector_grad,
    )
    masters = (student_square, student_qkv, student_expand, student_contract, student_vectors)
    firsts = (first_square, first_qkv, first_expand, first_contract, first_vectors)
    seconds = (second_square, second_qkv, second_expand, second_contract, second_vectors)
    results = [loss_sum, masked_count, grad_norm]
    for index, (master, first, second, grad) in enumerate(zip(masters, firsts, seconds, grads)):
        rate, decay = (rate_vector, 0.0) if index == 4 else (rate_matrix, decay_matrix)
        results += adam_update(master, first, second, grad * factor, rate, decay)
    return tuple(results)


def solution(mesh):
    return jax.shard_map(
        on_device,
        mesh=mesh,
        in_specs=(
            P(("batch", "mlp"), None, None),
            P(("batch", "mlp"), None),
            P(None, "batch", None),
            P("batch", None),
            P("batch", None),
            P("batch", None),
            P(None, "batch"),
            P(None, "batch", None),
            P("batch", None),
            P("batch", None),
            P("batch", None),
            P(None, "batch"),
            P(None, "batch", None),
            P("batch", None),
            P("batch", None),
            P("batch", None),
            P(None, "batch"),
            P(),
            P(),
            P(None, "mlp"),
            P("mlp", None),
            P(),
        ),
        out_specs=(
            P(),
            P(),
            P(),
            P(None, "batch", None),
            P(None, "batch", None),
            P(None, "batch", None),
            P("batch", None),
            P("batch", None),
            P("batch", None),
            P("batch", None),
            P("batch", None),
            P("batch", None),
            P("batch", None),
            P("batch", None),
            P("batch", None),
            P(None, "batch"),
            P(None, "batch"),
            P(None, "batch"),
        ),
        check_vma=False,
    )
```

time: 1480 us -> 515 us (0.35)
  waiting for transfers between devices: 996 us -> 120 us
  Pallas kernels: 0 us -> 199 us
  matrix products: 187 us -> 0 us
  blocking collectives: 104 us -> 0 us
  starting transfers between devices: 0.5 us -> 53.9 us
  local copies, waits for them, and re-layouts: 77.1 us -> 43.6 us
    reduce_scatter x4 -> x0, waiting for transfers between devices: 533 us -> none  [the longest x1 166 us: on_device(): lax.psum_scatter(local[2], 'batch', scatter_dimension=0, tiled=True)]
    all_gather x5 -> x2, waiting for transfers between devices: 230 us -> 0.02 us  [the longest x1 0.02 us: on_device(): lax.all_gather(half_of(student_expand, core, 1).astype(bf16), 'batch', ax...]
    pallas_call x0 -> x11, Pallas kernels: none -> 199 us  [call(): pl.pallas_call(kernel, grid_spec=pltpu.PrefetchScalarGridSpec(num_scalar_...]
    dot_general x28 -> x0, matrix products: 178 us -> none  [the longest x10 74.1 us: product(): return jnp.dot(left, right, preferred_element_type=jnp.float32)]
    unnamed x14 -> x2, waiting for transfers between devices: 158 us -> 0.03 us
    ppermute x0 -> x55, waiting for transfers between devices: none -> 120 us  [swap(): lax.ppermute(values, ('batch', 'mlp'), [(i, i ^ bit) for i in range(total)])]
    psum x1 -> x0, waiting for transfers between devices: 75.1 us -> none  [on_device(): lax.psum((shared[0], shared[1], shared[2], shared[3], shared[4]), 'mlp')]
    psum x3 -> x0, blocking collectives: 72 us -> none  [the longest x1 39.6 us: on_device(): loss_sum = lax.psum(loss_part, ('batch', 'mlp'))]
  transfers between devices with their start and end apart: 12 -> 57, of which waited for: 12 -> 25; matrix products, arithmetic and copies ran while one was open for 10% -> 19% of each run, Pallas kernels for 0% -> 31%
where the time goes in v1:
time: 515 us; the launch traced here: 505 us
  Pallas kernels  199 us (39%)
  waiting for transfers between devices  120 us (23%)
  other arithmetic  68.5 us (13%)
  starting transfers between devices  53.9 us (10%)
  local copies, waits for them, and re-layouts  43.6 us (8%)
  between operations  20.2 us (4%)
    pallas_call x11, Pallas kernels, call(): pl.pallas_call(kernel, grid_spec=pltpu.PrefetchScalarGridSpec(num_scalar_...  199 us
    ppermute x55, waiting for transfers between devices, swap(): lax.ppermute(values, ('batch', 'mlp'), [(i, i ^ bit) for i in range(total)])  120 us
    ppermute x55, starting transfers between devices, swap(): lax.ppermute(values, ('batch', 'mlp'), [(i, i ^ bit) for i in range(total)])  53.8 us
    sub x5, other arithmetic, adam_update(): master - step_rate * (corrected / (jnp.sqrt(scaled) + adam_eps) + weight_...  13.5 us
    select_n x22, other arithmetic, power_of_two(): result = jnp.where(size >> bit & 1 == 1, result * factor, result)  12.5 us
    slice x4, local copies, waits for them, and re-layouts, first_axis_half(): lax.index_in_dim(sums, 0, place, keepdims=False)  11.5 us
  transfers between devices with their start and end apart: 57, of which 25 were waited for; matrix products, arithmetic and copies ran while one was open for 19% of the time, Pallas kernels for 31%

profile of v1, /device:TPU:0, one launch (start us, length us, event | category | flops | bytes accessed | tf_op | source)
XLA Modules:
  0.0 505.0 jit_solution(1221235736388449099)
XLA Ops:
  29.2 15.2 %attend_teacher.2 = f32[416,768]{1,0:T(8,128)} custom-call(bf16[832,768]{1,0:T(8,128)(2,1)} %bitcast.188, bf16[768,768]{1,0:T(8,128)(2,1)} %get-tuple-element.219.refs_1_, bf16[768,2304]{1,0:T(8,128)(2,1)} %refs_2_.5, bf16[768,768]{1,0:T(8,128)(2,1)} %get-tuple-element.218.refs_3_, f32[13,768]{1,0:T(8,128)} %refs_2_.7), custom_call_target="tpu_custom_call" | custom-call | flops 14949999616 | bytes 1 | tf_op jit(solution)/shard_map/attend_teacher/pallas_call | solution.py:459
  48.5 15.3 %attend_teacher.3 = f32[416,768]{1,0:T(8,128)} custom-call(bf16[832,768]{1,0:T(8,128)(2,1)} %bitcast.189, bf16[768,768]{1,0:T(8,128)(2,1)} %get-tuple-element.219.refs_1_, bf16[768,2304]{1,0:T(8,128)(2,1)} %refs_2_.5, bf16[768,768]{1,0:T(8,128)(2,1)} %get-tuple-element.218.refs_3_, f32[13,768]{1,0:T(8,128)} %refs_2_.7), custom_call_target="tpu_custom_call" | custom-call | flops 14949999616 | bytes 1 | tf_op jit(solution)/shard_map/attend_teacher/pallas_call | solution.py:459
  63.8 3.0 pad_maximum_fusion.refs_0_
  66.8 21.5 %collective-permute-done.4 = bf16[2,96,1152]{2,1,0:T(8,128)(2,1)} collective-permute-done((bf16[2,96,1152]{2,1,0:T(8,128)(2,1)S(1)}, bf16[2,96,1152]{2,1,0:T(8,128)(2,1)}, u32[]{:S(2)}, u32[]{:S(2)}) %collective-permute-start.4) | collective-permute-done | bytes 442400 | tf_op jit(solution)/shard_map/ppermute | solution.py:673
  91.5 9.6 %teacher_ffn.2.refs_5_ = f32[832,768]{1,0:T(8,128)} custom-call(f32[832,768]{1,0:T(8,128)} %pad_maximum_fusion.refs_0_, f32[2,768]{1,0:T(2,128)} %pad_maximum_fusion.25.refs_1_, f32[13,768]{1,0:T(8,128)} %refs_2_.7, bf16[768,1536]{1,0:T(8,128)(2,1)} %constant_dynamic-update-slice_fusion.refs_3_, bf16[768,1536]{1,0:T(8,128)(2,1)} %collective-permute-done.9.refs_4_), custom_call_target="tpu_custom_call" | custom-call | flops 10350000128 | bytes 1 | tf_op jit(solution)/shard_map/teacher_ffn/pallas_call | solution.py:459
  101.2 13.0 %collective-permute-done.10.refs_5_.refs_7_ = bf16[4,96,1152]{2,1,0:T(8,128)(2,1)} collective-permute-done((bf16[4,96,1152]{2,1,0:T(8,128)(2,1)S(1)}, bf16[4,96,1152]{2,1,0:T(8,128)(2,1)}, u32[]{:S(2)}, u32[]{:S(2)}) %collective-permute-start.10) | collective-permute-done | bytes 884768 | tf_op jit(solution)/shard_map/ppermute | solution.py:673
  114.2 8.8 %collective-permute-done.11.refs_9_.refs_11_ = bf16[4,96,1152]{2,1,0:T(8,128)(2,1)} collective-permute-done((bf16[4,96,1152]{2,1,0:T(8,128)(2,1)S(1)}, bf16[4,96,1152]{2,1,0:T(8,128)(2,1)}, u32[]{:S(2)}, u32[]{:S(2)}) %collective-permute-start.11) | collective-permute-done | bytes 884768 | tf_op jit(solution)/shard_map/ppermute | solution.py:673
  130.5 29.3 %attend_student.1 = (f32[832,768]{1,0:T(8,128)}, f32[832,768]{1,0:T(8,128)}, bf16[832,2304]{1,0:T(8,128)(2,1)}, bf16[832,2304]{1,0:T(8,128)(2,1)}) custom-call(s32[19]{0:T(128)} %stack.58.refs_0_, bf16[832,768]{1,0:T(8,128)(2,1)} %bitcast.190, f32[832,128]{1,0:T(8,128)} %broadcast_in_dim.1043.refs_2_.refs_4_, f32[17,768]{1,0:T(8,128)} %bitcast.200, ...), custom_call_target="tpu_custom_call" | custom-call | flops 33350000640 | bytes 1 | tf_op jit(solution)/shard_map/attend_student/pallas_call | solution.py:459
  161.3 5.5 %collective-permute-done.7 = f32[1,128]{1,0:T(1,128)S(1)} collective-permute-done((f32[1,128]{1,0:T(1,128)S(1)}, f32[1,128]{1,0:T(1,128)S(1)}, u32[]{:S(2)}, u32[]{:S(2)}) %collective-permute-start.7) | collective-permute-done | bytes 544 | tf_op jit(solution)/shard_map/ppermute | solution.py:673
  171.1 10.1 %teacher_ffn.3.refs_3_ = f32[832,768]{1,0:T(8,128)} custom-call(f32[832,768]{1,0:T(8,128)} %pad_maximum_fusion.refs_0_, f32[2,768]{1,0:T(2,128)} %pad_maximum_fusion.26.refs_1_, f32[13,768]{1,0:T(8,128)} %refs_2_.7, bf16[768,1536]{1,0:T(8,128)(2,1)} %collective-permute-done.16.refs_3_, bf16[768,1536]{1,0:T(8,128)(2,1)} %collective-permute-done.17.refs_4_, ...), custom_call_target="tpu_custom_call" | custom-call | flops 10350000128 | bytes 1 | tf_op jit(solution)/shard_map/teacher_ffn/pallas_call | solution.py:459
  182.6 34.2 %student_ffn.1 = (bf16[832,2304]{1,0:T(8,128)(2,1)}, bf16[832,3456]{1,0:T(8,128)(2,1)}, bf16[832,3456]{1,0:T(8,128)(2,1)}, f32[832,768]{1,0:T(8,128)}, f32[16,768]{1,0:T(8,128)}) custom-call(s32[19]{0:T(128)} %stack.58.refs_0_, f32[1]{0:T(128)} %bitcast.15.refs_1_, f32[832,768]{1,0:T(8,128)} %get-tuple-element.94.refs_2_, f32[832,768]{1,0:T(8,128)} %teacher_ffn.3.refs_3_, ...), custom_call_target="tpu_custom_call" | custom-call | flops 40249999360 | bytes 1 | tf_op jit(solution)/shard_map/student_ffn/pallas_call | solution.py:459
  217.5 9.1 %collective-permute-done.21.refs_2_.refs_4_ = bf16[832,3456]{1,0:T(8,128)(2,1)} collective-permute-done((bf16[832,3456]{1,0:T(8,128)(2,1)}, bf16[832,3456]{1,0:T(8,128)(2,1)}, u32[]{:S(2)}, u32[]{:S(2)}) %collective-permute-start.21) | collective-permute-done | bytes 5750816 | tf_op jit(solution)/shard_map/ppermute | solution.py:673
  226.6 15.0 %grad_expand.1 = (f32[8,2,48,1920]{3,2,1,0:T(8,128)}, f32[8,1920]{1,0:T(8,128)}) custom-call(s32[19]{0:T(128)} %stack.58.refs_0_, bf16[832,3456]{1,0:T(8,128)(2,1)} %get-tuple-element.103.refs_1_, bf16[832,3456]{1,0:T(8,128)(2,1)} %collective-permute-done.21.refs_2_.refs_4_, bf16[832,2304]{1,0:T(8,128)(2,1)} %get-tuple-element.101.refs_3_.refs_1_, ...), custom_call_target="tpu_custom_call" | custom-call | flops 17250000896 | bytes 1 | tf_op jit(solution)/shard_map/grad_expand/pallas_call | solution.py:459
  241.6 3.1 fusion.96
  249.5 13.7 %grad_contract.1 = (f32[8,2,192,384]{3,2,1,0:T(8,128)}, f32[8,384]{1,0:T(8,128)}) custom-call(s32[19]{0:T(128)} %stack.58.refs_0_, bf16[832,2304]{1,0:T(8,128)(2,1)} %get-tuple-element.101.refs_3_.refs_1_, bf16[832,3456]{1,0:T(8,128)(2,1)} %collective-permute-done.20.refs_2_.refs_4_, bf16[832,3456]{1,0:T(8,128)(2,1)} %get-tuple-element.102.refs_3_, ...), custom_call_target="tpu_custom_call" | custom-call | flops 14949999616 | bytes 1 | tf_op jit(solution)/shard_map/grad_contract/pallas_call | solution.py:459
  263.2 4.3 fusion.97
  271.2 35.8 %attend_back.1 = (bf16[832,1920]{1,0:T(8,128)(2,1)}, bf16[832,1920]{1,0:T(8,128)(2,1)}, f32[16,768]{1,0:T(8,128)}) custom-call(s32[19]{0:T(128)} %stack.58.refs_0_, f32[832,768]{1,0:T(8,128)} %get-tuple-element.109.refs_1_, bf16[832,2304]{1,0:T(8,128)(2,1)} %get-tuple-element.110.refs_2_, f32[832,768]{1,0:T(8,128)} %get-tuple-element.111.refs_3_, ...), custom_call_target="tpu_custom_call" | custom-call | flops 41400000512 | bytes 1 | tf_op jit(solution)/shard_map/attend_back/pallas_call | solution.py:459
  322.7 6.0 %collective-permute-done.28 = f16[784,384]{1,0:T(8,128)(2,1)} collective-permute-done((f16[784,384]{1,0:T(8,128)(2,1)S(1)}, f16[784,384]{1,0:T(8,128)(2,1)}, u32[]{:S(2)}, u32[]{:S(2)}) %collective-permute-start.28) | collective-permute-done | bytes 602144 | tf_op jit(solution)/shard_map/ppermute | solution.py:673
  332.3 8.9 %collective-permute-done.25 = f16[208,1920]{1,0:T(8,128)(2,1)S(1)} collective-permute-done((f16[208,1920]{1,0:T(8,128)(2,1)}, f16[208,1920]{1,0:T(8,128)(2,1)S(1)}, u32[]{:S(2)}, u32[]{:S(2)}) %collective-permute-start.25) | collective-permute-done | bytes 798752 | tf_op jit(solution)/shard_map/ppermute | solution.py:673
  342.8 8.8 %grad_out_joint.1 = (f32[8,2,48,768]{3,2,1,0:T(8,128)}, f32[8,768]{1,0:T(8,128)}) custom-call(s32[19]{0:T(128)} %stack.58.refs_0_, bf16[832,2304]{1,0:T(8,128)(2,1)} %get-tuple-element.117.refs_1_, bf16[832,2304]{1,0:T(8,128)(2,1)} %collective-permute-done.26.refs_2_, bf16[832,1920]{1,0:T(8,128)(2,1)} %get-tuple-element.113.refs_3_, ...), custom_call_target="tpu_custom_call" | custom-call | flops 10350000128 | bytes 1 | tf_op jit(solution)/shard_map/grad_out_joint/pallas_call | solution.py:459
  359.0 11.7 %grad_joint_embed.1 = (f32[8,2,48,1152]{3,2,1,0:T(8,128)}, f32[8,1152]{1,0:T(8,128)}) custom-call(s32[19]{0:T(128)} %stack.58.refs_0_, bf16[832,2304]{1,0:T(8,128)(2,1)} %get-tuple-element.117.refs_1_, bf16[832,2304]{1,0:T(8,128)(2,1)} %collective-permute-done.26.refs_2_, bf16[832,1920]{1,0:T(8,128)(2,1)} %get-tuple-element.113.refs_3_, ...), custom_call_target="tpu_custom_call" | custom-call | flops 12650000384 | bytes 1 | tf_op jit(solution)/shard_map/grad_joint_embed/pallas_call | solution.py:459
  380.5 3.1 collective-permute-start.34
  396.6 14.3 %collective-permute-done.42 = f16[208,384]{1,0:T(8,128)(2,1)S(1)} collective-permute-done((f16[208,384]{1,0:T(8,128)(2,1)S(1)}, f16[208,384]{1,0:T(8,128)(2,1)S(1)}, u32[]{:S(2)}, u32[]{:S(2)}) %collective-permute-start.42) | collective-permute-done | bytes 159776 | tf_op jit(solution)/shard_map/ppermute | solution.py:673
  416.1 2.8 collective-permute-start.38
  420.9 6.3 %collective-permute-done.38 = f16[112,768]{1,0:T(8,128)(2,1)S(1)} collective-permute-done((f16[112,768]{1,0:T(8,128)(2,1)S(1)}, f16[112,768]{1,0:T(8,128)(2,1)S(1)}, u32[]{:S(2)}, u32[]{:S(2)}) %collective-permute-start.38) | collective-permute-done | bytes 172064 | tf_op jit(solution)/shard_map/ppermute | solution.py:673
  430.5 2.8 collective-permute-done.43
  434.1 6.5 %collective-permute-done.39 = f16[208,1152]{1,0:T(8,128)(2,1)S(1)} collective-permute-done((f16[208,1152]{1,0:T(8,128)(2,1)S(1)}, f16[208,1152]{1,0:T(8,128)(2,1)S(1)}, u32[]{:S(2)}, u32[]{:S(2)}) %collective-permute-start.39) | collective-permute-done | bytes 479264 | tf_op jit(solution)/shard_map/ppermute | solution.py:673
  443.0 3.4 collective-permute-start.40
  450.4 3.3 collective-permute-start.45
  462.7 3.3 collective-permute-done.46
  482.4 4.2 multiply_subtract_fusion.1
  486.7 3.9 multiply_subtract_fusion
  (387 shorter events, 148.9 us)
Async XLA Ops:
  7.2 152.7 %all-gather.3.cloned.1.call-start = ((), (), s32[]{:S(2)}) async-start(), calls=%async_computation | async-start | bytes 2654208 | tf_op jit(solution)/shard_map/all_gather | solution.py:868
  9.1 151.0 %all-gather.5.cloned.1.call-start = ((), (), s32[]{:S(2)}) async-start(), calls=%async_computation.1 | async-start | bytes 2654208 | tf_op jit(solution)/shard_map/all_gather | solution.py:871
  12.9 78.6 %collective-permute-start.9 = (bf16[768,1536]{1,0:T(8,128)(2,1)}, bf16[768,1536]{1,0:T(8,128)(2,1)}, u32[]{:S(2)}, u32[]{:S(2)}) collective-permute-start(bf16[768,1536]{1,0:T(8,128)(2,1)} %constant_dynamic-update-slice_fusion.refs_3_), channel_id=1, source_target_pairs={{0,1},{1,0},{2,3},{3,2},{4,5},{5,4},{6,7},{7,6},{8,9},{9,8},{10,11... | collective-permute-start | bytes 7077896 | tf_op jit(solution)/shard_map/ppermute | solution.py:673
  13.4 112.1 %collective-permute-start.16 = (bf16[768,1536]{1,0:T(8,128)(2,1)}, bf16[768,1536]{1,0:T(8,128)(2,1)}, u32[]{:S(2)}, u32[]{:S(2)}) collective-permute-start(bf16[768,1536]{1,0:T(8,128)(2,1)} %constant_dynamic-update-slice_fusion.refs_3_), channel_id=1, source_target_pairs={{0,2},{1,3},{2,0},{3,1},{4,6},{5,7},{6,4},{7,5},{8,10},{9,11},{10,... | collective-permute-start | bytes 7077896 | tf_op jit(solution)/shard_map/ppermute | solution.py:673
  18.8 27.0 %collective-permute-start.2 = (f32[18,768]{1,0:T(8,128)S(1)}, f32[18,768]{1,0:T(8,128)S(1)}, u32[]{:S(2)}, u32[]{:S(2)}) collective-permute-start(f32[18,768]{1,0:T(8,128)S(1)} %concatenate.206), channel_id=1, source_target_pairs={{0,4},{1,5},{2,6},{3,7},{4,0},{5,1},{6,2},{7,3},{8,12},{9,13},{10,... | collective-permute-start | bytes 165896 | tf_op jit(solution)/shard_map/ppermute | solution.py:673
  20.5 25.4 %collective-permute-start.1 = (bf16[1,96,1152]{2,1,0:T(8,128)(2,1)S(1)}, bf16[1,96,1152]{2,1,0:T(8,128)(2,1)S(1)}, u32[]{:S(2)}, u32[]{:S(2)}) collective-permute-start(bf16[1,96,1152]{2,1,0:T(8,128)(2,1)S(1)} %fusion.20), channel_id=1, source_target_pairs={{0,4},{1,5},{2,6},{3,7},{4,0},{5,1},{6,2},{7,3},{8,12},{9,13},{10,... | collective-permute-start | bytes 663560 | tf_op jit(solution)/shard_map/ppermute | solution.py:673
  20.9 25.0 %collective-permute-start = (bf16[1,96,1152]{2,1,0:T(8,128)(2,1)S(1)}, bf16[1,96,1152]{2,1,0:T(8,128)(2,1)S(1)}, u32[]{:S(2)}, u32[]{:S(2)}) collective-permute-start(bf16[1,96,1152]{2,1,0:T(8,128)(2,1)S(1)} %pad_maximum_fusion.17), channel_id=1, source_target_pairs={{0,16},{1,17},{2,18},{3,19},{4,20},{5,21},{6,22},{7,23},{8,24},{9,... | collective-permute-start | bytes 663560 | tf_op jit(solution)/shard_map/ppermute | solution.py:673
  46.0 20.7 %collective-permute-start.5 = (f32[18,768]{1,0:T(8,128)S(1)}, f32[18,768]{1,0:T(8,128)S(1)}, u32[]{:S(2)}, u32[]{:S(2)}) collective-permute-start(f32[18,768]{1,0:T(8,128)S(1)} %add.276), channel_id=1, source_target_pairs={{0,8},{1,9},{2,10},{3,11},{4,12},{5,13},{6,14},{7,15},{8,0},{9,1},... | collective-permute-start | bytes 165896 | tf_op jit(solution)/shard_map/ppermute | solution.py:673
  47.8 40.5 %collective-permute-start.4 = (bf16[2,96,1152]{2,1,0:T(8,128)(2,1)S(1)}, bf16[2,96,1152]{2,1,0:T(8,128)(2,1)}, u32[]{:S(2)}, u32[]{:S(2)}) collective-permute-start(bf16[2,96,1152]{2,1,0:T(8,128)(2,1)S(1)} %pad_maximum_fusion.11), channel_id=1, source_target_pairs={{0,16},{1,17},{2,18},{3,19},{4,20},{5,21},{6,22},{7,23},{8,24},{9,... | collective-permute-start | bytes 1327112 | tf_op jit(solution)/shard_map/ppermute | solution.py:673
  48.1 41.3 %collective-permute-start.3 = (bf16[2,96,1152]{2,1,0:T(8,128)(2,1)S(1)}, bf16[2,96,1152]{2,1,0:T(8,128)(2,1)S(1)}, u32[]{:S(2)}, u32[]{:S(2)}) collective-permute-start(bf16[2,96,1152]{2,1,0:T(8,128)(2,1)S(1)} %pad_maximum_fusion.10), channel_id=1, source_target_pairs={{0,8},{1,9},{2,10},{3,11},{4,12},{5,13},{6,14},{7,15},{8,0},{9,1},... | collective-permute-start | bytes 1327112 | tf_op jit(solution)/shard_map/ppermute | solution.py:673
  89.5 24.7 %collective-permute-start.10 = (bf16[4,96,1152]{2,1,0:T(8,128)(2,1)S(1)}, bf16[4,96,1152]{2,1,0:T(8,128)(2,1)}, u32[]{:S(2)}, u32[]{:S(2)}) collective-permute-start(bf16[4,96,1152]{2,1,0:T(8,128)(2,1)S(1)} %pad_maximum_fusion.4.refs_4_.refs_6_), channel_id=1, source_target_pairs={{0,4},{1,5},{2,6},{3,7},{4,0},{5,1},{6,2},{7,3},{8,12},{9,13},{10,... | collective-permute-start | bytes 2654216 | tf_op jit(solution)/shard_map/ppermute | solution.py:673
  91.1 32.0 %collective-permute-start.11 = (bf16[4,96,1152]{2,1,0:T(8,128)(2,1)S(1)}, bf16[4,96,1152]{2,1,0:T(8,128)(2,1)}, u32[]{:S(2)}, u32[]{:S(2)}) collective-permute-start(bf16[4,96,1152]{2,1,0:T(8,128)(2,1)S(1)} %pad_maximum_fusion.5.refs_8_.refs_10_), channel_id=1, source_target_pairs={{0,8},{1,9},{2,10},{3,11},{4,12},{5,13},{6,14},{7,15},{8,0},{9,1},... | collective-permute-start | bytes 2654216 | tf_op jit(solution)/shard_map/ppermute | solution.py:673
  91.1 32.5 %collective-permute-start.6 = (f32[18,768]{1,0:T(8,128)S(1)}, f32[18,768]{1,0:T(8,128)S(1)}, u32[]{:S(2)}, u32[]{:S(2)}) collective-permute-start(f32[18,768]{1,0:T(8,128)S(1)} %add.277), channel_id=1, source_target_pairs={{0,16},{1,17},{2,18},{3,19},{4,20},{5,21},{6,22},{7,23},{8,24},{9,... | collective-permute-start | bytes 165896 | tf_op jit(solution)/shard_map/ppermute | solution.py:673
  125.4 45.7 %collective-permute-start.17 = (bf16[768,1536]{1,0:T(8,128)(2,1)}, bf16[768,1536]{1,0:T(8,128)(2,1)}, u32[]{:S(2)}, u32[]{:S(2)}) collective-permute-start(bf16[768,1536]{1,0:T(8,128)(2,1)} %collective-permute-done.16.refs_3_), channel_id=1, source_target_pairs={{0,1},{1,0},{2,3},{3,2},{4,5},{5,4},{6,7},{7,6},{8,9},{9,8},{10,11... | collective-permute-start | bytes 7077896 | tf_op jit(solution)/shard_map/ppermute | solution.py:673
  159.9 21.3 %collective-permute-start.18 = (bf16[1,768,1536]{2,1,0:T(8,128)(2,1)}, bf16[1,768,1536]{2,1,0:T(8,128)(2,1)S(1)}, u32[]{:S(2)}, u32[]{:S(2)}) collective-permute-start(bf16[1,768,1536]{2,1,0:T(8,128)(2,1)} %bitcast.204), channel_id=1, source_target_pairs={{0,1},{1,0},{2,3},{3,2},{4,5},{5,4},{6,7},{7,6},{8,9},{9,8},{10,11... | collective-permute-start | bytes 7077896 | tf_op jit(solution)/shard_map/ppermute | solution.py:673
  160.1 21.1 %collective-permute-start.19 = (bf16[1,3072,384]{2,1,0:T(8,128)(2,1)}, bf16[1,3072,384]{2,1,0:T(8,128)(2,1)}, u32[]{:S(2)}, u32[]{:S(2)}) collective-permute-start(bf16[1,3072,384]{2,1,0:T(8,128)(2,1)} %bitcast.206), channel_id=1, source_target_pairs={{0,1},{1,0},{2,3},{3,2},{4,5},{5,4},{6,7},{7,6},{8,9},{9,8},{10,11... | collective-permute-start | bytes 7077896 | tf_op jit(solution)/shard_map/ppermute | solution.py:673
  216.9 32.6 %collective-permute-start.20 = (bf16[832,3456]{1,0:T(8,128)(2,1)}, bf16[832,3456]{1,0:T(8,128)(2,1)}, u32[]{:S(2)}, u32[]{:S(2)}) collective-permute-start(bf16[832,3456]{1,0:T(8,128)(2,1)} %get-tuple-element.102.refs_3_), channel_id=1, source_target_pairs={{0,1},{1,0},{2,3},{3,2},{4,5},{5,4},{6,7},{7,6},{8,9},{9,8},{10,11... | collective-permute-start | bytes 17252360 | tf_op jit(solution)/shard_map/ppermute | solution.py:673
  217.4 125.4 %collective-permute-start.26 = (bf16[832,2304]{1,0:T(8,128)(2,1)}, bf16[832,2304]{1,0:T(8,128)(2,1)}, u32[]{:S(2)}, u32[]{:S(2)}) collective-permute-start(bf16[832,2304]{1,0:T(8,128)(2,1)} %get-tuple-element.117.refs_1_), channel_id=1, source_target_pairs={{0,1},{1,0},{2,3},{3,2},{4,5},{5,4},{6,7},{7,6},{8,9},{9,8},{10,11... | collective-permute-start | bytes 11501576 | tf_op jit(solution)/shard_map/ppermute | solution.py:673
  248.9 65.4 %collective-permute-start.22 = (f16[400,1920]{1,0:T(8,128)(2,1)}, f16[400,1920]{1,0:T(8,128)(2,1)}, u32[]{:S(2)}, u32[]{:S(2)}) collective-permute-start(f16[400,1920]{1,0:T(8,128)(2,1)} %pad_maximum_fusion.1), channel_id=1, source_target_pairs={{0,4},{1,5},{2,6},{3,7},{4,0},{5,1},{6,2},{7,3},{8,12},{9,13},{10,... | collective-permute-start | bytes 4608008 | tf_op jit(solution)/shard_map/ppermute | solution.py:673
  270.9 36.9 %collective-permute-start.23 = (f16[1552,384]{1,0:T(8,128)(2,1)}, f16[1552,384]{1,0:T(8,128)(2,1)}, u32[]{:S(2)}, u32[]{:S(2)}) collective-permute-start(f16[1552,384]{1,0:T(8,128)(2,1)} %pad_maximum_fusion.2), channel_id=1, source_target_pairs={{0,2},{1,3},{2,0},{3,1},{4,6},{5,7},{6,4},{7,5},{8,10},{9,11},{10,... | collective-permute-start | bytes 3575816 | tf_op jit(solution)/shard_map/ppermute | solution.py:673
  307.0 35.8 %collective-permute-start.27 = (bf16[832,1920]{1,0:T(8,128)(2,1)}, bf16[832,1920]{1,0:T(8,128)(2,1)}, u32[]{:S(2)}, u32[]{:S(2)}) collective-permute-start(bf16[832,1920]{1,0:T(8,128)(2,1)} %get-tuple-element.118), channel_id=1, source_target_pairs={{0,1},{1,0},{2,3},{3,2},{4,5},{5,4},{6,7},{7,6},{8,9},{9,8},{10,11... | collective-permute-start | bytes 9584648 | tf_op jit(solution)/shard_map/ppermute | solution.py:673
  321.1 20.2 %collective-permute-start.25 = (f16[208,1920]{1,0:T(8,128)(2,1)}, f16[208,1920]{1,0:T(8,128)(2,1)S(1)}, u32[]{:S(2)}, u32[]{:S(2)}) collective-permute-start(f16[208,1920]{1,0:T(8,128)(2,1)} %pad_maximum_fusion.6), channel_id=1, source_target_pairs={{0,8},{1,9},{2,10},{3,11},{4,12},{5,13},{6,14},{7,15},{8,0},{9,1},... | collective-permute-start | bytes 2396168 | tf_op jit(solution)/shard_map/ppermute | solution.py:673
  355.9 35.8 %collective-permute-start.32 = (f16[400,768]{1,0:T(8,128)(2,1)}, f16[400,768]{1,0:T(8,128)(2,1)}, u32[]{:S(2)}, u32[]{:S(2)}) collective-permute-start(f16[400,768]{1,0:T(8,128)(2,1)} %pad_maximum_fusion.7), channel_id=1, source_target_pairs={{0,4},{1,5},{2,6},{3,7},{4,0},{5,1},{6,2},{7,3},{8,12},{9,13},{10,... | collective-permute-start | bytes 1843208 | tf_op jit(solution)/shard_map/ppermute | solution.py:673
  357.4 20.9 %collective-permute-start.31 = (f16[400,384]{1,0:T(8,128)(2,1)}, f16[400,384]{1,0:T(8,128)(2,1)}, u32[]{:S(2)}, u32[]{:S(2)}) collective-permute-start(f16[400,384]{1,0:T(8,128)(2,1)} %pad_maximum_fusion.15), channel_id=1, source_target_pairs={{0,8},{1,9},{2,10},{3,11},{4,12},{5,13},{6,14},{7,15},{8,0},{9,1},... | collective-permute-start | bytes 921608 | tf_op jit(solution)/shard_map/ppermute | solution.py:673
  359.0 24.6 %collective-permute-start.30 = (f16[112,1920]{1,0:T(8,128)(2,1)}, f16[112,1920]{1,0:T(8,128)(2,1)}, u32[]{:S(2)}, u32[]{:S(2)}) collective-permute-start(f16[112,1920]{1,0:T(8,128)(2,1)} %pad_maximum_fusion.12), channel_id=1, source_target_pairs={{0,16},{1,17},{2,18},{3,19},{4,20},{5,21},{6,22},{7,23},{8,24},{9,... | collective-permute-start | bytes 1290248 | tf_op jit(solution)/shard_map/ppermute | solution.py:673
  376.9 36.6 %collective-permute-start.36 = (f16[400,1152]{1,0:T(8,128)(2,1)S(1)}, f16[400,1152]{1,0:T(8,128)(2,1)S(1)}, u32[]{:S(2)}, u32[]{:S(2)}) collective-permute-start(f16[400,1152]{1,0:T(8,128)(2,1)S(1)} %pad_maximum_fusion.3), channel_id=1, source_target_pairs={{0,2},{1,3},{2,0},{3,1},{4,6},{5,7},{6,4},{7,5},{8,10},{9,11},{10,... | collective-permute-start | bytes 2764808 | tf_op jit(solution)/shard_map/ppermute | solution.py:673
  386.5 25.3 %collective-permute-start.41 = (f16[112,1920]{1,0:T(8,128)(2,1)S(1)}, f16[112,1920]{1,0:T(8,128)(2,1)S(1)}, u32[]{:S(2)}, u32[]{:S(2)}) collective-permute-start(f16[112,1920]{1,0:T(8,128)(2,1)S(1)} %pad_maximum_fusion.13), channel_id=1, source_target_pairs={{0,2},{1,3},{2,0},{3,1},{4,6},{5,7},{6,4},{7,5},{8,10},{9,11},{10,... | collective-permute-start | bytes 1290248 | tf_op jit(solution)/shard_map/ppermute | solution.py:673
  389.8 21.1 %collective-permute-start.42 = (f16[208,384]{1,0:T(8,128)(2,1)S(1)}, f16[208,384]{1,0:T(8,128)(2,1)S(1)}, u32[]{:S(2)}, u32[]{:S(2)}) collective-permute-start(f16[208,384]{1,0:T(8,128)(2,1)S(1)} %pad_maximum_fusion.21), channel_id=1, source_target_pairs={{0,2},{1,3},{2,0},{3,1},{4,6},{5,7},{6,4},{7,5},{8,10},{9,11},{10,... | collective-permute-start | bytes 479240 | tf_op jit(solution)/shard_map/ppermute | solution.py:673
  394.4 21.2 %collective-permute-start.35 = (f16[208,768]{1,0:T(8,128)(2,1)S(1)}, f16[208,768]{1,0:T(8,128)(2,1)S(1)}, u32[]{:S(2)}, u32[]{:S(2)}) collective-permute-start(f16[208,768]{1,0:T(8,128)(2,1)S(1)} %pad_maximum_fusion.14), channel_id=1, source_target_pairs={{0,8},{1,9},{2,10},{3,11},{4,12},{5,13},{6,14},{7,15},{8,0},{9,1},... | collective-permute-start | bytes 958472 | tf_op jit(solution)/shard_map/ppermute | solution.py:673
  411.8 74.9 %collective-permute-start.54 = (f32[384,384]{1,0:T(8,128)S(1)}, f32[384,384]{1,0:T(8,128)}, u32[]{:S(2)}, u32[]{:S(2)}) collective-permute-start(f32[384,384]{1,0:T(8,128)S(1)} %get-tuple-element.169), channel_id=1, source_target_pairs={{0,1},{1,0},{2,3},{3,2},{4,5},{5,4},{6,7},{7,6},{8,9},{9,8},{10,11... | collective-permute-start | bytes 1769480 | tf_op jit(solution)/shard_map/ppermute | solution.py:673
  413.0 57.2 %collective-permute-start.53 = (f32[96,1920]{1,0:T(8,128)S(1)}, f32[96,1920]{1,0:T(8,128)}, u32[]{:S(2)}, u32[]{:S(2)}) collective-permute-start(f32[96,1920]{1,0:T(8,128)S(1)} %bitcast.173), channel_id=1, source_target_pairs={{0,1},{1,0},{2,3},{3,2},{4,5},{5,4},{6,7},{7,6},{8,9},{9,8},{10,11... | collective-permute-start | bytes 2211848 | tf_op jit(solution)/shard_map/ppermute | solution.py:673
  434.1 27.9 %collective-permute-start.52 = (f32[96,768]{1,0:T(8,128)S(1)}, f32[96,768]{1,0:T(8,128)S(1)}, u32[]{:S(2)}, u32[]{:S(2)}) collective-permute-start(f32[96,768]{1,0:T(8,128)S(1)} %bitcast.192), channel_id=1, source_target_pairs={{0,1},{1,0},{2,3},{3,2},{4,5},{5,4},{6,7},{7,6},{8,9},{9,8},{10,11... | collective-permute-start | bytes 884744 | tf_op jit(solution)/shard_map/ppermute | solution.py:673
  (64 other events, 458.6 us)
Sparse Core Ops, SparseCore 0:
  10.8 77.9 all-gather.2
  91.5 56.3 all-gather.4
